TPU v7x, 32 devices: a whole 2x2x4 slice. The times are simulated.
32 devices in a mesh: facet: 8 (over z, x), strip: 4 (over y, core).
Axes of the slice: x: 2, y: 2, z: 4, core: 2. Of those that a mesh axis runs over, the one named last changes fastest.
Arguments:
- facets: bfloat16 [8, 2, 512, 8192], P('facet', None, None, 'strip'), may hold values from -6 to 6
- offsets: int32 [4], replicated, may hold values from 0 to 32767
- visibilities: float32 [2, 512, 2048], P(None, 'strip', 'facet'), may hold values from -24 to 24
- weights: float32 [512, 2048], P('strip', 'facet'), may hold values from 0.1 to 1
- mask: int32 [512, 2048], P('strip', 'facet'), may hold values 0 or 1
Outputs:
- facet_update: bfloat16 [8, 2, 512, 8192], P('facet', None, None, 'strip')
Inputs may be any that keep to these rules, and one draw needn't show every extreme that they name: `mask`: 1 where the cell holds a sampled visibility.
All inputs are finite; a program needn't handle non-finite values. No bound on the sum of `mask` on one device may be relied on, other than what follows from the above.
Results may differ from a plain program's by a relative error of at most 0.0058.
Values may be sent and summed in bfloat16 or wider, within the bound.
No kernel may reach another device: no remote copies, remote signals or barrier semaphores. Data moves between devices by JAX's collectives and lax.ppermute only.
A program may use at most 128 MiB of HBM per device.

v0:
```python
import math

import jax
import jax.numpy as jnp
from jax import lax
from jax.sharding import PartitionSpec as P

NG = 32768
XM = 8192
SG = 512
NSUB = 4
FROWS = 4


def residue_angle(count):
    return count.astype(jnp.float32) * (2.0 * math.pi / NG)


def dft_kernel(rows):
    positions = jnp.arange(rows, dtype=jnp.int32)
    cells = jnp.arange(SG, dtype=jnp.int32)
    angle = residue_angle(positions[:, None] * cells[None, :] % NG)
    return jnp.concatenate([jnp.cos(angle), jnp.sin(angle)], axis=1).astype(jnp.bfloat16)


def row_angles(start, rows, offsets):
    positions = start + jnp.arange(rows, dtype=jnp.int32)
    return residue_angle(offsets[:, None] * positions[None, :] % NG)


def column_angles(facet_index, offsets):
    centre = (facet_index % FROWS * XM + NG // 2) % NG
    cells = jnp.arange(SG, dtype=jnp.int32)
    return residue_angle((cells[None, :] * centre % NG + offsets[:, None] * centre % NG) % NG)


def forward(data, start, facet_index, offsets, kernel_table):
    columns = data.shape[1]
    rows = data.shape[2]
    phi = row_angles(start, rows, offsets)[:, None, :]
    cos_phi = jnp.cos(phi)
    sin_phi = jnp.sin(phi)
    real_part = data[0].astype(jnp.float32)[None]
    imag_part = data[1].astype(jnp.float32)[None]
    twisted = jnp.stack(
        [real_part * cos_phi + imag_part * sin_phi, imag_part * cos_phi - real_part * sin_phi],
        axis=1,
    ).astype(jnp.bfloat16)
    spectra = jnp.dot(twisted.reshape(-1, rows), kernel_table, preferred_element_type=jnp.float32)
    spectra = spectra.reshape(NSUB, 2, columns, 2, SG)
    spectrum_real = spectra[:, 0, :, 0] + spectra[:, 1, :, 1]
    spectrum_imag = spectra[:, 1, :, 0] - spectra[:, 0, :, 1]
    psi = column_angles(facet_index, offsets)[:, None, :]
    cos_psi = jnp.cos(psi)
    sin_psi = jnp.sin(psi)
    scale = 1.0 / math.sqrt(XM)
    result_real = (spectrum_real * cos_psi + spectrum_imag * sin_psi) * scale
    result_imag = (spectrum_imag * cos_psi - spectrum_real * sin_psi) * scale
    stacked = jnp.stack([result_real, result_imag])
    return stacked.transpose(0, 2, 1, 3).reshape(2, columns, NSUB * SG)


def adjoint(residual, start, facet_index, offsets, kernel_table):
    columns = residual.shape[1]
    rows = kernel_table.shape[0]
    values = residual.astype(jnp.float32).reshape(2, columns, NSUB, SG).transpose(0, 2, 1, 3)
    psi = column_angles(facet_index, offsets)[:, None, :]
    cos_psi = jnp.cos(psi)
    sin_psi = jnp.sin(psi)
    first = values[0] * cos_psi - values[1] * sin_psi
    second = values[1] * cos_psi + values[0] * sin_psi
    untwisted = jnp.stack([first, second], axis=1).astype(jnp.bfloat16)
    images = jnp.einsum(
        "mj,xpj->pmx",
        untwisted.reshape(-1, SG),
        kernel_table.reshape(rows, 2, SG),
        preferred_element_type=jnp.float32,
    )
    images = images.reshape(2, NSUB, 2, columns, rows)
    image_real = images[0, :, 0] - images[1, :, 1]
    image_imag = images[0, :, 1] + images[1, :, 0]
    phi = row_angles(start, rows, offsets)[:, None, :]
    cos_phi = jnp.cos(phi)
    sin_phi = jnp.sin(phi)
    scale = 1.0 / math.sqrt(XM)
    total_real = jnp.sum(image_real * cos_phi - image_imag * sin_phi, axis=0) * scale
    total_imag = jnp.sum(image_imag * cos_phi + image_real * sin_phi, axis=0) * scale
    return jnp.stack([total_real, total_imag])


def weigh(model, visibilities, weights, mask):
    factor = weights * mask.astype(jnp.float32)
    return (factor[None] * (visibilities - model)).astype(jnp.bfloat16)


def on_device(facets, offsets, visibilities, weights, mask):
    facet_index = lax.axis_index("facet")
    regrouped = lax.all_to_all(facets[0], "strip", split_axis=1, concat_axis=2, tiled=True)
    kernel_table = dft_kernel(regrouped.shape[2])
    contribution = forward(regrouped, 0, facet_index, offsets, kernel_table)
    model = lax.psum_scatter(contribution, "facet", scatter_dimension=2, tiled=True)
    residual = weigh(model, visibilities, weights, mask)
    gathered = lax.all_gather(residual, "facet", axis=2, tiled=True)
    update = adjoint(gathered, 0, facet_index, offsets, kernel_table).astype(jnp.bfloat16)
    result = lax.all_to_all(update, "strip", split_axis=2, concat_axis=1, tiled=True)
    return result[None]


def solution(mesh):
    placed = (
        P("facet", None, None, "strip"),
        P(),
        P(None, "strip", "facet"),
        P("strip", "facet"),
        P("strip", "facet"),
    )
    return jax.shard_map(
        on_device,
        mesh=mesh,
        in_specs=placed,
        out_specs=P("facet", None, None, "strip"),
        check_vma=False,
    )
```

profile of v0, /device:TPU:0, one launch (start us, length us, event | category | flops | bytes accessed | tf_op | source)
XLA Modules:
  0.0 451.6 jit_solution(7619882456607674424)
XLA Ops:
  6.5 0.0 copy-start.3
  6.5 8.5 %copy.105 = bf16[1,2,512,2048]{3,1,2,0:T(2,128)(2,1)} copy(bf16[1,2,512,2048]{3,2,1,0:T(8,128)(2,1)} %param.5) | data formatting | bytes 8388608 | tf_op args[0]
  15.1 4.9 %all-to-all-start = ((bf16[2,512,2048]{2,0,1:T(2,128)(2,1)}), bf16[2,512,2048]{2,0,1:T(2,128)(2,1)}, u32[]{:S(2)}, u32[]{:S(2)}) async-start(bf16[2,512,2048]{2,0,1:T(2,128)(2,1)} %bitcast.137), calls=%async_computation | async-start | bytes 8388608 | tf_op jit(solution)/shard_map/all_to_all | solution.py:98
  19.9 0.2 reduce-scatter.2.cloned.1.call-start
  20.2 67.2 %sine_convert_fusion = (bf16[8192,512]{0,1:T(8,128)(2,1)}, bf16[8192,512]{0,1:T(8,128)(2,1)}) fusion(), kind=kLoop, calls=%fused_computation.31 | loop fusion | flops 67108864 | bytes 16777216 | tf_op jit(solution)/shard_map/convert.11
  87.4 0.0 copy-done.3
  87.4 0.2 fusion.37
  87.6 13.7 %pad_maximum_fusion = bf16[8192,1024]{0,1:T(8,128)(2,1)} fusion(bf16[8192,512]{0,1:T(8,128)(2,1)} %get-tuple-element.19, bf16[8192,512]{0,1:T(8,128)(2,1)} %get-tuple-element.20), kind=kLoop, calls=%fused_computation.28 | loop fusion | flops 33554432 | bytes 33554432 | tf_op jit(solution)/shard_map/concatenate | solution.py:23
  101.3 1.2 fusion.32
  102.5 0.0 all-to-all-done
  102.5 4.1 copy.77
  106.6 4.4 slice_convert_fusion.1
  111.0 5.3 %copy.78 = f32[1,128,4,2048]{1,3,2,0:T(8,128)} copy(f32[1,128,4,2048]{3,1,2,0:T(8,128)} %get-tuple-element.11) | data formatting | bytes 8388608 | tf_op jit(solution)/shard_map/convert_element_type | solution.py:43
  116.3 5.6 %copy.79 = f32[128,8192]{1,0:T(8,128)} copy(f32[128,8192]{0,1:T(8,128)} %bitcast.138) | data formatting | bytes 8388608 | tf_op jit(solution)/shard_map/convert_element_type | solution.py:43
  121.9 5.3 %copy.80 = f32[1,128,4,2048]{1,3,2,0:T(8,128)} copy(f32[1,128,4,2048]{3,1,2,0:T(8,128)} %get-tuple-element.12) | data formatting | bytes 8388608 | tf_op jit(solution)/shard_map/convert_element_type | solution.py:44
  127.3 5.6 %copy.81 = f32[128,8192]{1,0:T(8,128)} copy(f32[128,8192]{0,1:T(8,128)} %bitcast.139) | data formatting | bytes 8388608 | tf_op jit(solution)/shard_map/convert_element_type | solution.py:44
  132.9 6.5 %add_convert_fusion = (bf16[4,1,128,8192]{3,2,1,0:T(8,128)(2,1)S(1)}, bf16[4,1,128,8192]{3,2,1,0:T(8,128)(2,1)S(1)}) fusion(f32[4,8192]{1,0:T(4,128)S(1)} %get-tuple-element.18, f32[128,8192]{1,0:T(8,128)} %copy.81, f32[4,8192]{1,0:T(4,128)S(1)} %get-tuple-element.17, f32[128,8192]{1,0:T(8,128)} %copy.79), kind=kLoop, calls=%fused_computation.36 | loop fusion | flops 33554432 | bytes 25427968 | tf_op jit(solution)/shard_map/convert.12
  139.4 21.8 %fusion.14 = f32[4,2,128,2,512]{4,2,3,1,0:T(8,128)S(1)} fusion(bf16[2,512,8192,1,1]{2,1,0,4,3:T(8,128)(2,1)} %bitcast.136, bf16[4,1,128,8192]{3,2,1,0:T(8,128)(2,1)S(1)} %get-tuple-element.8, bf16[4,1,128,8192]{3,2,1,0:T(8,128)(2,1)S(1)} %get-tuple-element.7), kind=kOutput, calls=%fused_computation.25 | convolution fusion | flops 17213423616 | bytes 37748736 | tf_op jit(solution)/shard_map/dot_general | solution.py:49
  161.2 0.0 copy-start.1
  161.2 0.0 copy-start.2
  161.2 0.0 copy-start
  161.2 0.7 add_multiply_fusion
  161.9 0.2 maximum_bitcast_fusion.2
  162.1 1.8 copy.84
  163.9 0.0 reduce-scatter.2.cloned.1.call-update
  164.0 0.3 all-gather.2.cloned.1.call-start
  164.2 0.0 copy-done.1
  164.2 0.0 copy-done.2
  164.3 0.1 copy.75
  164.4 0.0 copy-done
  164.4 0.1 copy.85
  164.5 70.9 %reduce-scatter.2.cloned.1.call-done = f32[2,128,256]{1,2,0:T(8,128)} async-done(((f32[2,128,2048]{1,2,0:T(8,128)}), f32[2,128,256]{1,2,0:T(8,128)}) %reduce-scatter.2.cloned.1.call-update) | async-done | bytes 262160 | tf_op jit(solution)/shard_map/reduce_scatter | solution.py:101
  235.4 1.6 multiply_convert_fusion.2
  237.0 0.0 all-gather.2.cloned.1.call-update
  237.0 68.4 %sine_convert_fusion.1 = (bf16[8192,1,512]{2,0,1:T(8,128)(2,1)}, bf16[8192,1,512]{2,0,1:T(8,128)(2,1)}) fusion(), kind=kLoop, calls=%fused_computation.37 | loop fusion | flops 67108864 | bytes 16777216 | tf_op jit(solution)/shard_map/convert.15
  305.4 0.0 all-gather.2.cloned.1.call-done
  305.4 1.5 copy.86
  306.9 0.3 subtract_convert_fusion.1
  307.2 0.1 pad_maximum_fusion.2
  307.3 31.5 %fusion.10 = f32[8192,2,1024]{0,2,1:T(8,128)} fusion(bf16[1024,512,1]{1,0,2:T(8,128)(2,1)S(1)} %bitcast.144, bf16[8192,1,512]{2,0,1:T(8,128)(2,1)} %get-tuple-element.21, bf16[8192,1,512]{2,0,1:T(8,128)(2,1)} %get-tuple-element.22), kind=kOutput, calls=%fused_computation.20 | convolution fusion | flops 17188257792 | bytes 84934656 | tf_op jit(solution)/shard_map/mj,xpj->pmx/dot_general | solution.py:73
  338.8 26.7 %subtract_reduce_fusion = (f32[128,8192]{1,0:T(8,128)}, f32[128,8192]{1,0:T(8,128)}) fusion(f32[4,8192]{1,0:T(4,128)S(1)} %get-tuple-element.18, f32[4,8192]{1,0:T(4,128)S(1)} %get-tuple-element.17, f32[2,4,2,128,8192]{4,3,2,1,0:T(8,128)} %bitcast.25), kind=kLoop, calls=%fused_computation.30 | loop fusion | flops 39845888 | bytes 75759616 | tf_op jit(solution)/shard_map/reduce_sum | solution.py:86
  365.5 2.6 fusion.23
  368.0 2.6 fusion.24
  370.6 2.4 pad_maximum_fusion.1
  373.0 11.1 %copy.93 = bf16[2,128,8192]{1,0,2:T(2,128)(2,1)} copy(bf16[2,128,8192]{2,1,0:T(8,128)(2,1)} %pad_maximum_fusion.1) | data formatting | bytes 8388608 | tf_op jit(solution)/shard_map/stack | solution.py:88
  384.1 51.9 %all_to_all.30 = bf16[2,128,8192]{1,0,2:T(2,128)(2,1)S(1)} all-to-all(bf16[2,128,8192]{1,0,2:T(2,128)(2,1)} %copy.93), channel_id=1, replica_groups=mesh['facet'=8,'strip'=4] {'strip'}, dimensions={2} | all-to-all | bytes 8388608 | tf_op jit(solution)/shard_map/all_to_all | solution.py:105
  436.0 2.5 copy.94
  438.5 6.2 %copy.95 = bf16[2,4,128,2048]{3,2,1,0:T(8,128)(2,1)} copy(bf16[2,4,128,2048]{2,3,1,0:T(8,128)(2,1)} %bitcast.140) | data formatting | bytes 8388608 | tf_op jit(solution)/shard_map/all_to_all | solution.py:105
  (3 shorter events, 0.0 us)
Async XLA Ops:
  6.5 80.9 %copy-start.3 = (s32[4]{0:T(128)S(1)}, s32[4]{0:T(128)}, u32[]{:S(2)}) copy-start(s32[4]{0:T(128)} %param.6) | copy-start | bytes 52
  15.1 87.5 %all-to-all-start = ((bf16[2,512,2048]{2,0,1:T(2,128)(2,1)}), bf16[2,512,2048]{2,0,1:T(2,128)(2,1)}, u32[]{:S(2)}, u32[]{:S(2)}) async-start(bf16[2,512,2048]{2,0,1:T(2,128)(2,1)} %bitcast.137), calls=%async_computation | async-start | bytes 8388608 | tf_op jit(solution)/shard_map/all_to_all | solution.py:98
  19.9 215.4 %reduce-scatter.2.cloned.1.call-start = ((), (), s32[]{:S(2)}) async-start(), calls=%async_computation.3 | async-start | bytes 2359296 | tf_op jit(solution)/shard_map/reduce_scatter | solution.py:101
  161.2 3.0 copy-start.1
  161.2 3.0 copy-start.2
  161.2 3.1 copy-start
  164.0 141.5 %all-gather.2.cloned.1.call-start = ((), (), s32[]{:S(2)}) async-start(), calls=%async_computation.4 | async-start | bytes 1179648 | tf_op jit(solution)/shard_map/all_gather | solution.py:103
Sparse Core Ops, SparseCore 0:
  164.1 71.2 reduce-scatter.1
  237.6 39.2 all-gather.1
where the time goes:
time: 453 us; the launch traced here: 452 us
  other arithmetic  199 us (44%)
  waiting for transfers between devices  70.9 us (16%)
  local copies, waits for them, and re-layouts  57.8 us (13%)
  matrix products  53.2 us (12%)
  blocking collectives  51.9 us (11%)
  between operations  13.6 us (3%)
  starting transfers between devices  5.36 us (1%)
    another operation x4, other arithmetic  142 us
    reduce_scatter x1, waiting for transfers between devices, on_device(): lax.psum_scatter(contribution, 'facet', scatter_dimension=2, tiled=True)  70.9 us
    all_to_all x1, blocking collectives, on_device(): lax.all_to_all(update, 'strip', split_axis=2, concat_axis=1, tiled=True)  51.9 us
    dot_general x1, matrix products, adjoint(): jnp.einsum('mj,xpj->pmx', untwisted.reshape(-1, SG), kernel_table.reshape...  31.5 us
    reduce_sum x1, other arithmetic, adjoint(): jnp.sum(image_real * cos_phi - image_imag * sin_phi, axis=0) * scale  26.7 us
    dot_general x1, matrix products, forward(): jnp.dot(twisted.reshape(-1, rows), kernel_table, preferred_element_type=j...  21.8 us
    concatenate x1, other arithmetic, dft_kernel(): jnp.concatenate([jnp.cos(angle), jnp.sin(angle)], axis=1)  13.7 us
    another operation x1, local copies, waits for them, and re-layouts, adjoint(): return jnp.stack([total_real, total_imag])  11.1 us
  transfers between devices with their start and end apart: 3, of which 1 were waited for; matrix products, arithmetic and copies ran while one was open for 33% of the time, Pallas kernels for 0%

commit v1 on v0

v1 whole, which is shorter than its diff:
```python
import functools
import math

import jax
import jax.numpy as jnp
from jax import lax
from jax.experimental import pallas as pl
from jax.experimental.pallas import tpu as pltpu
from jax.sharding import PartitionSpec as P

NG = 32768
FROWS = 4
FINE = 32
AXES = ("facet", "strip")
bf16 = jnp.bfloat16
f32 = jnp.float32


def unit_circle(count):
    count = count & (NG - 1)
    quarter = (count + NG // 8) >> (NG.bit_length() - 3)
    angle = (count - quarter * (NG // 4)).astype(f32) * (2.0 * math.pi / NG)
    square = angle * angle
    sine = angle * (
        1.0 + square * (-1.0 / 6 + square * (1.0 / 120 + square * (-1.0 / 5040 + square * (1.0 / 362880))))
    )
    cosine = 1.0 + square * (
        -0.5 + square * (1.0 / 24 + square * (-1.0 / 720 + square * (1.0 / 40320 + square * (-1.0 / 3628800))))
    )
    odd = (quarter & 1) == 1
    first = jnp.where(odd, sine, cosine)
    second = jnp.where(odd, cosine, sine)
    return (
        jnp.where(((quarter + 1) & 2) != 0, -first, first),
        jnp.where((quarter & 2) != 0, -second, second),
    )


class Layout:
    def __init__(self, mesh):
        self.strips = mesh.shape["strip"]
        self.facets = mesh.shape["facet"]
        self.cores = 2 if self.strips % 2 == 0 else 1
        self.high = self.strips // self.cores
        self.near = 2 if self.facets % 2 == 0 else 1
        self.far = self.facets // self.near
        self.mixed = self.high == self.near and self.cores == 2

    def place(self):
        strip = lax.axis_index("strip")
        facet = lax.axis_index("facet")
        return strip // self.cores, strip % self.cores, facet // self.near, facet % self.near

    def permutation(self, move):
        pairs = []
        for facet in range(self.facets):
            for strip in range(self.strips):
                digits = move(strip // self.cores, strip % self.cores, facet // self.near, facet % self.near)
                high, core, far, near = digits
                target = (far * self.near + near) * self.strips + high * self.cores + core
                pairs.append((facet * self.strips + strip, target))
        return pairs

    def along(self, stage, shift):
        def move(high, core, far, near):
            if stage == "core":
                return high, (core + shift) % self.cores, far, near
            if stage == "far":
                return high, core, (far + shift) % self.far, near
            first = "near" if self.mixed and core == 1 else "high"
            second = "high" if first == "near" else "near"
            if (first if stage == "first" else second) == "high":
                return (high + shift) % self.high, core, far, near
            return high, core, far, (near + shift) % self.near

        return self.permutation(move)

    def send(self, value, stage, shift):
        return lax.ppermute(value, AXES, self.along(stage, shift))


def forward_kernel(lay, scale, info, *refs):
    if lay.cores == 2:
        away_in, keep_in, away_out, keep_out, cos_ref, sin_ref = refs
        halves = ((away_in, away_out, 1 - info[1]), (keep_in, keep_out, info[1]))
    else:
        keep_in, keep_out, cos_ref, sin_ref = refs
        halves = ((keep_in, keep_out, info[1]),)
    tile = pl.program_id(0)
    rows, width = cos_ref.shape
    cells = (pl.num_programs(0) * width) // info_offsets(info)
    start = tile * width
    offset = info[2 + start // cells]
    frequency = offset + start % cells + lax.broadcasted_iota(jnp.int32, (1, width), 1)
    coarse_rows = info[0] + FINE * lax.broadcasted_iota(jnp.int32, (rows // FINE, 1), 0)
    fine_rows = lax.broadcasted_iota(jnp.int32, (FINE, 1), 0)
    frequency = frequency & (NG - 1)
    coarse_cos, coarse_sin = unit_circle((coarse_rows & (NG - 1)) * frequency)
    fine_cos, fine_sin = unit_circle(fine_rows * frequency)
    for block in range(rows // FINE):
        c = coarse_cos[block : block + 1]
        s = coarse_sin[block : block + 1]
        cos_ref[block * FINE : (block + 1) * FINE] = (c * fine_cos - s * fine_sin).astype(bf16)
        sin_ref[block * FINE : (block + 1) * FINE] = (s * fine_cos + c * fine_sin).astype(bf16)
    near = lax.rem(tile, lay.near)
    for data, out, core in halves:
        high, depth = data.shape[1], data.shape[-2]
        values = data[...].reshape(2 * high * depth, rows)
        with_cos = jnp.dot(values, cos_ref[...], preferred_element_type=f32).reshape(2, high, depth, width)
        with_sin = jnp.dot(values, sin_ref[...], preferred_element_type=f32).reshape(2, high, depth, width)
        real = ((with_cos[0] + with_sin[1]) * scale).astype(bf16)
        imag = ((with_cos[1] - with_sin[0]) * scale).astype(bf16)
        for h in range(high):
            spot = h * lay.near + near
            if lay.mixed:
                spot = jnp.where(core == 1, near * lay.high + h, spot)
            out[spot, 0, 0] = real[h]
            out[spot, 0, 1] = imag[h]


def info_offsets(info):
    return info.shape[0] - 2


def forward(lay, data, info, chunk, chunks, width, scale):
    rows = data.shape[-1]
    depth = data.shape[3] // chunks
    tiles = lay.facets
    half = (2, lay.high, None, depth, rows)
    out_block = (lay.high * lay.near, 1, 2, depth, width)
    out_shape = jax.ShapeDtypeStruct((lay.high * lay.near, lay.far, 2, depth, width), bf16)
    out_spec = pl.BlockSpec(out_block, lambda t, info: (0, t // lay.near, 0, 0, 0))
    table_shape = jax.ShapeDtypeStruct((rows, tiles * width), bf16)
    table_spec = pl.BlockSpec((rows, width), lambda t, info: (0, t))
    in_specs = [pl.BlockSpec(half, lambda t, info: (0, 0, info[1], chunk, 0))]
    if lay.cores == 2:
        in_specs.insert(0, pl.BlockSpec(half, lambda t, info: (0, 0, 1 - info[1], chunk, 0)))
    n = len(in_specs)
    return pl.pallas_call(
        functools.partial(forward_kernel, lay, scale),
        out_shape=(out_shape,) * n + (table_shape,) * 2,
        grid_spec=pltpu.PrefetchScalarGridSpec(
            num_scalar_prefetch=1,
            grid=(tiles,),
            in_specs=in_specs,
            out_specs=(out_spec,) * n + (table_spec,) * 2,
        ),
        compiler_params=pltpu.CompilerParams(vmem_limit_bytes=58 << 20),
        name="forward",
    )(info, *([data] * n))


def adjoint_kernel(lay, scale, place, *refs):
    sources = refs[: lay.cores]
    cos_ref, sin_ref, out_ref, left = refs[lay.cores :]
    width = sources[0].shape[-1]
    depth = sources[0].shape[-2]

    @pl.when(pl.program_id(0) == 0)
    def _():
        for i, source in enumerate(sources):
            core = place[1] if i == 0 else 1 - place[1]
            for first in range(source.shape[0]):
                for second in range(source.shape[1]):
                    shifts = (first, second)
                    high = lax.rem(place[0] - shifts[0] + lay.high, lay.high)
                    near = lax.rem(place[3] - shifts[1] + lay.near, lay.near)
                    if lay.mixed:
                        high = jnp.where(core == 1, lax.rem(place[0] - second + lay.high, lay.high), high)
                        near = jnp.where(core == 1, lax.rem(place[3] - first + lay.near, lay.near), near)
                    for third in range(lay.far):
                        far = lax.rem(place[2] - third + lay.far, lay.far)
                        spot = pl.multiple_of((far * lay.near + near) * width, width)
                        for part in range(2):
                            left[i, part, high, :, pl.ds(spot, width)] = source[first, second, third, part]

    for i in range(len(sources)):
        core = place[1] if i == 0 else 1 - place[1]
        values = left[i].reshape(2 * lay.high * depth, left.shape[-1])
        contract = (((1,), (1,)), ((), ()))
        with_cos = lax.dot_general(values, cos_ref[...], contract, preferred_element_type=f32)
        with_sin = lax.dot_general(values, sin_ref[...], contract, preferred_element_type=f32)
        shape = (2, lay.high, depth, with_cos.shape[-1])
        with_cos, with_sin = with_cos.reshape(shape), with_sin.reshape(shape)
        real = ((with_cos[0] - with_sin[1]) * scale).astype(bf16)
        imag = ((with_cos[1] + with_sin[0]) * scale).astype(bf16)
        for h in range(lay.high):
            out_ref[0, h, core] = real[h]
            out_ref[1, h, core] = imag[h]


def adjoint(lay, sources, cos_table, sin_table, place, shape, chunk, chunks, scale):
    rows, total = cos_table.shape
    depth = shape[3] // chunks
    tile = 256 if rows % 256 == 0 else rows
    source_spec = pl.BlockSpec(sources[0].shape, lambda t, place: (0,) * 6)
    table_spec = pl.BlockSpec((tile, total), lambda t, place: (t, 0))
    return pl.pallas_call(
        functools.partial(adjoint_kernel, lay, scale),
        out_shape=jax.ShapeDtypeStruct(shape, bf16),
        grid_spec=pltpu.PrefetchScalarGridSpec(
            num_scalar_prefetch=1,
            grid=(rows // tile,),
            in_specs=[source_spec] * len(sources) + [table_spec] * 2,
            out_specs=pl.BlockSpec((2, lay.high, lay.cores, depth, tile), lambda t, place: (0, 0, 0, chunk, t)),
            scratch_shapes=[pltpu.VMEM((len(sources), 2, lay.high, depth, total), bf16)],
        ),
        compiler_params=pltpu.CompilerParams(vmem_limit_bytes=58 << 20),
        name="adjoint",
    )(place, *sources, cos_table, sin_table)


def pick(value, index):
    return lax.dynamic_index_in_dim(value, index, 0, keepdims=False)


def total_of(*values):
    return functools.reduce(jnp.add, [v.astype(f32) for v in values])


def scatter_stage(lay, value, stage, size, mine):
    received = [
        lay.send(pick(value, lax.rem(mine + shift, size)), stage, shift) for shift in range(1, size)
    ]
    return total_of(pick(value, mine), *received)


def gather_stage(lay, value, stage, size):
    return jnp.stack([value] + [lay.send(value, stage, shift) for shift in range(1, size)])


def on_device(lay, facets, offsets, visibilities, weights, mask):
    high, core, far, near = lay.place()
    _, _, columns, rows = facets.shape
    width = visibilities.shape[2]
    own_columns = visibilities.shape[1]
    facet_index = lax.axis_index("facet")
    all_rows = rows * lay.strips
    base = lax.axis_index("strip") * rows + facet_index % FROWS * all_rows + NG // 2
    info = jnp.concatenate([jnp.stack([base, core]).astype(jnp.int32), offsets])
    place = jnp.stack([high, core, far, near]).astype(jnp.int32)
    scale = 1.0 / math.sqrt(all_rows)
    data = facets.reshape(2, lay.high, lay.cores, own_columns, rows)
    *partial, cos_table, sin_table = forward(lay, data, info, 0, 1, width, scale)
    value = partial[-1]
    if lay.cores == 2:
        value = total_of(value, lay.send(partial[0], "core", 1)).astype(bf16)
    sizes = (lay.high, lay.near)
    digits = (high, near)
    if lay.mixed:
        digits = (jnp.where(core == 1, near, high), jnp.where(core == 1, high, near))
    value = value.reshape(*sizes, *value.shape[1:])
    value = scatter_stage(lay, value, "first", sizes[0], digits[0]).astype(bf16)
    value = scatter_stage(lay, value, "second", sizes[1], digits[1]).astype(bf16)
    model = scatter_stage(lay, value, "far", lay.far, far)
    factor = weights * mask.astype(f32)
    residual = (factor[None] * (visibilities - model)).astype(bf16)
    value = gather_stage(lay, residual, "far", lay.far)
    value = gather_stage(lay, value, "second", sizes[1])
    value = gather_stage(lay, value, "first", sizes[0])
    sources = [value]
    if lay.cores == 2:
        sources.append(lay.send(value, "core", 1))
    update = adjoint(lay, sources, cos_table, sin_table, place, data.shape, 0, 1, scale)
    return update.reshape(facets.shape)


def solution(mesh):
    placed = (
        P("facet", None, None, "strip"),
        P(),
        P(None, "strip", "facet"),
        P("strip", "facet"),
        P("strip", "facet"),
    )
    return jax.shard_map(
        functools.partial(on_device, Layout(mesh)),
        mesh=mesh,
        in_specs=placed,
        out_specs=P("facet", None, None, "strip"),
        check_vma=False,
    )
```

time: 453 us -> 143 us (0.32)
  other arithmetic: 199 us -> 7.12 us
  local copies, waits for them, and re-layouts: 57.8 us -> 2.82 us
  matrix products: 53.2 us -> 0 us
  blocking collectives: 51.9 us -> 0 us
  Pallas kernels: 0 us -> 48.6 us
  between operations: 13.6 us -> 0.12 us
  starting transfers between devices: 5.36 us -> 16.8 us
    another operation x6 -> x4, other arithmetic: 145 us -> 1.1 us  [the longest x1 0.68 us: on_device(): place = jnp.stack([high, core, far, near]).astype(jnp.int32)]
    reduce_scatter x1 -> x0, waiting for transfers between devices: 70.9 us -> none  [on_device(): lax.psum_scatter(contribution, 'facet', scatter_dimension=2, tiled=True)]
    ppermute x0 -> x12, waiting for transfers between devices: none -> 67.4 us  [send(): return lax.ppermute(value, AXES, self.along(stage, shift))]
    dot_general x2 -> x0, matrix products: 53.2 us -> none  [the longest x1 31.5 us: adjoint(): jnp.einsum('mj,xpj->pmx', untwisted.reshape(-1, SG), kernel_table.reshape...]
    all_to_all x1 -> x0, blocking collectives: 51.9 us -> none  [on_device(): lax.all_to_all(update, 'strip', split_axis=2, concat_axis=1, tiled=True)]
    pallas_call x0 -> x2, Pallas kernels: none -> 48.6 us  [the longest x1 24.4 us: forward(): pl.pallas_call(functools.partial(forward_kernel, lay, scale), out_shape=(...]
    reduce_sum x1 -> x0, other arithmetic: 26.7 us -> none  [adjoint(): jnp.sum(image_real * cos_phi - image_imag * sin_phi, axis=0) * scale]
    convert_element_type x4 -> x0, local copies, waits for them, and re-layouts: 21.9 us -> none  [the longest x2 11 us: forward(): real_part = data[0].astype(jnp.float32)[None]]
  transfers between devices with their start and end apart: 3 -> 12, of which waited for: 1 -> 10; matrix products, arithmetic and copies ran while one was open for 33% -> 0% of each run, Pallas kernels for 0% -> 0%
where the time goes in v1:
time: 143 us
  waiting for transfers between devices  67.4 us (47%)
  Pallas kernels  48.6 us (34%)
  starting transfers between devices  16.8 us (12%)
  other arithmetic  7.12 us (5%)
  local copies, waits for them, and re-layouts  2.82 us (2%)
    ppermute x12, waiting for transfers between devices, send(): return lax.ppermute(value, AXES, self.along(stage, shift))  67.4 us
    pallas_call x1, Pallas kernels, forward(): pl.pallas_call(functools.partial(forward_kernel, lay, scale), out_shape=(...  24.4 us
    pallas_call x1, Pallas kernels, adjoint(): pl.pallas_call(functools.partial(adjoint_kernel, lay, scale), out_shape=j...  24.2 us
    ppermute x12, starting transfers between devices, send(): return lax.ppermute(value, AXES, self.along(stage, shift))  16.8 us
    convert_element_type x1, other arithmetic, on_device(): value = total_of(value, lay.send(partial[0], 'core', 1)).astype(bf16)  2.98 us
  transfers between devices with their start and end apart: 12, of which 10 were waited for; matrix products, arithmetic and copies ran while one was open for 0% of the time, Pallas kernels for 0%

profile of v1, /device:TPU:0, one launch (start us, length us, event | category | flops | bytes accessed | tf_op | source)
XLA Modules:
  0.0 142.8 jit_solution(14258296187414916959)
XLA Ops:
  0.0 1.3 pad_add_fusion.1.info
  1.3 24.4 %forward.1 = (bf16[4,4,2,128,256]{4,3,2,1,0:T(8,128)(2,1)}, bf16[4,4,2,128,256]{4,3,2,1,0:T(8,128)(2,1)}, bf16[2048,2048]{1,0:T(8,128)(2,1)}, bf16[2048,2048]{1,0:T(8,128)(2,1)}) custom-call(s32[6]{0:T(128)} %pad_add_fusion.1.info, bf16[2,2,2,128,2048]{4,3,2,1,0:T(8,128)(2,1)} %bitcast.37, bf16[2,2,2,128,2048]{4,3,2,1,0:T(8,128)(2,1)} %bitcast.38), custom_call_target="tpu_custom_call" | custom-call | tf_op jit(solution)/shard_map/forward/pallas_call | solution.py:139
  25.7 0.5 collective-permute-start
  26.2 4.0 %collective-permute-done = bf16[4,4,2,128,256]{4,3,2,1,0:T(8,128)(2,1)S(1)} collective-permute-done((bf16[4,4,2,128,256]{4,3,2,1,0:T(8,128)(2,1)}, bf16[4,4,2,128,256]{4,3,2,1,0:T(8,128)(2,1)S(1)}, u32[]{:S(2)}, u32[]{:S(2)}) %collective-permute-start) | collective-permute-done | bytes 2097184 | tf_op jit(solution)/shard_map/ppermute | solution.py:79
  30.2 0.0 copy-start.1
  30.2 1.3 copy-done.1
  31.5 3.0 %add_convert_fusion = bf16[4,4,2,128,256]{4,3,2,1,0:T(8,128)(2,1)S(1)} fusion(bf16[4,4,2,128,256]{4,3,2,1,0:T(8,128)(2,1)} %copy-done.1, bf16[4,4,2,128,256]{4,3,2,1,0:T(8,128)(2,1)} %get-tuple-element.9), kind=kLoop, calls=%fused_computation | loop fusion | flops 4194304 | bytes 6291456 | tf_op jit(solution)/shard_map/convert_element_type | solution.py:247
  34.5 0.1 dynamic-slice_bitcast_fusion
  34.6 2.9 %collective-permute-start.1 = (bf16[2,4,2,128,256]{4,3,2,1,0:T(8,128)(2,1)S(1)}, bf16[2,4,2,128,256]{4,3,2,1,0:T(8,128)(2,1)}, u32[]{:S(2)}, u32[]{:S(2)}) collective-permute-start(bf16[2,4,2,128,256]{4,3,2,1,0:T(8,128)(2,1)S(1)} %dynamic-slice_bitcast_fusion), channel_id=1, source_target_pairs={{0,2},{1,5},{2,0},{3,7},{4,6},{5,1},{6,4},{7,3},{8,10},{9,13},{10,... | collective-permute-start | bytes 3145736 | tf_op jit(solution)/shard_map/ppermute | solution.py:79
  37.6 12.9 %collective-permute-done.1 = bf16[2,4,2,128,256]{4,3,2,1,0:T(8,128)(2,1)} collective-permute-done((bf16[2,4,2,128,256]{4,3,2,1,0:T(8,128)(2,1)S(1)}, bf16[2,4,2,128,256]{4,3,2,1,0:T(8,128)(2,1)}, u32[]{:S(2)}, u32[]{:S(2)}) %collective-permute-start.1) | collective-permute-done | bytes 1048608 | tf_op jit(solution)/shard_map/ppermute | solution.py:79
  50.4 1.5 %fusion = bf16[2,4,2,128,256]{4,3,2,1,0:T(8,128)(2,1)S(1)} fusion(bf16[2,4,2,128,256]{4,3,2,1,0:T(8,128)(2,1)} %collective-permute-done.1, bf16[2,2,4,2,128,256]{5,4,3,2,1,0:T(8,128)(2,1)S(1)} %bitcast.40, s32[]{:T(128)S(6)} %select_n.61), kind=kLoop, calls=%fused_computation.3 | loop fusion | flops 2097152 | bytes 3145732 | tf_op jit(solution)/shard_map/convert_element_type | solution.py:253
  52.0 0.0 copy-start.4
  52.0 0.0 copy-start.5
  52.0 0.0 copy-start.3
  52.1 2.1 %collective-permute-start.2 = (bf16[4,2,128,256]{3,2,1,0:T(8,128)(2,1)S(1)}, bf16[4,2,128,256]{3,2,1,0:T(8,128)(2,1)S(1)}, u32[]{:S(2)}, u32[]{:S(2)}) collective-permute-start(bf16[4,2,128,256]{3,2,1,0:T(8,128)(2,1)S(1)} %dynamic-slice_bitcast_fusion.1), channel_id=1, source_target_pairs={{0,4},{1,3},{2,6},{3,1},{4,0},{5,7},{6,2},{7,5},{8,12},{9,11},{10,... | collective-permute-start | bytes 1572872 | tf_op jit(solution)/shard_map/ppermute | solution.py:79
  54.1 7.2 %collective-permute-done.2 = bf16[4,2,128,256]{3,2,1,0:T(8,128)(2,1)S(1)} collective-permute-done((bf16[4,2,128,256]{3,2,1,0:T(8,128)(2,1)S(1)}, bf16[4,2,128,256]{3,2,1,0:T(8,128)(2,1)S(1)}, u32[]{:S(2)}, u32[]{:S(2)}) %collective-permute-start.2) | collective-permute-done | bytes 524320 | tf_op jit(solution)/shard_map/ppermute | solution.py:79
  61.3 0.1 fusion.1
  61.5 2.1 %collective-permute-start.3 = (bf16[2,128,256]{2,1,0:T(8,128)(2,1)S(1)}, bf16[2,128,256]{2,1,0:T(8,128)(2,1)S(1)}, u32[]{:S(2)}, u32[]{:S(2)}) collective-permute-start(bf16[2,128,256]{2,1,0:T(8,128)(2,1)S(1)} %get-tuple-element.17), channel_id=1, source_target_pairs={{0,8},{1,9},{2,10},{3,11},{4,12},{5,13},{6,14},{7,15},{8,16},{9,17... | collective-permute-start | bytes 393224 | tf_op jit(solution)/shard_map/ppermute | solution.py:79
  63.6 2.1 %collective-permute-start.5 = (bf16[2,128,256]{2,1,0:T(8,128)(2,1)S(1)}, bf16[2,128,256]{2,1,0:T(8,128)(2,1)S(1)}, u32[]{:S(2)}, u32[]{:S(2)}) collective-permute-start(bf16[2,128,256]{2,1,0:T(8,128)(2,1)S(1)} %get-tuple-element.18), channel_id=1, source_target_pairs={{0,24},{1,25},{2,26},{3,27},{4,28},{5,29},{6,30},{7,31},{8,0},{9,1... | collective-permute-start | bytes 393224 | tf_op jit(solution)/shard_map/ppermute | solution.py:79
  65.7 0.9 collective-permute-start.4
  66.7 0.0 copy-done.4
  66.7 0.0 copy-done.5
  66.7 3.4 %collective-permute-done.3 = bf16[2,128,256]{2,1,0:T(8,128)(2,1)S(1)} collective-permute-done((bf16[2,128,256]{2,1,0:T(8,128)(2,1)S(1)}, bf16[2,128,256]{2,1,0:T(8,128)(2,1)S(1)}, u32[]{:S(2)}, u32[]{:S(2)}) %collective-permute-start.3) | collective-permute-done | bytes 131104 | tf_op jit(solution)/shard_map/ppermute | solution.py:79
  70.1 0.0 collective-permute-done.5
  70.1 6.1 %collective-permute-done.4 = bf16[2,128,256]{2,1,0:T(8,128)(2,1)S(1)} collective-permute-done((bf16[2,128,256]{2,1,0:T(8,128)(2,1)S(1)}, bf16[2,128,256]{2,1,0:T(8,128)(2,1)S(1)}, u32[]{:S(2)}, u32[]{:S(2)}) %collective-permute-start.4) | collective-permute-done | bytes 131104 | tf_op jit(solution)/shard_map/ppermute | solution.py:79
  76.2 0.0 copy-done.3
  76.2 0.1 fusion.6
  76.3 2.3 %collective-permute-start.8 = (bf16[2,128,256]{2,1,0:T(8,128)(2,1)S(1)}, bf16[2,128,256]{2,1,0:T(8,128)(2,1)S(1)}, u32[]{:S(2)}, u32[]{:S(2)}) collective-permute-start(bf16[2,128,256]{2,1,0:T(8,128)(2,1)S(1)} %fusion.6), channel_id=1, source_target_pairs={{0,24},{1,25},{2,26},{3,27},{4,28},{5,29},{6,30},{7,31},{8,0},{9,1... | collective-permute-start | bytes 393224 | tf_op jit(solution)/shard_map/ppermute | solution.py:79
  78.5 0.0 collective-permute-start.7
  78.5 0.6 collective-permute-start.6
  79.2 3.2 %collective-permute-done.8 = bf16[2,128,256]{2,1,0:T(8,128)(2,1)S(1)} collective-permute-done((bf16[2,128,256]{2,1,0:T(8,128)(2,1)S(1)}, bf16[2,128,256]{2,1,0:T(8,128)(2,1)S(1)}, u32[]{:S(2)}, u32[]{:S(2)}) %collective-permute-start.8) | collective-permute-done | bytes 131104 | tf_op jit(solution)/shard_map/ppermute | solution.py:79
  82.4 6.1 %collective-permute-done.7 = bf16[2,128,256]{2,1,0:T(8,128)(2,1)S(1)} collective-permute-done((bf16[2,128,256]{2,1,0:T(8,128)(2,1)S(1)}, bf16[2,128,256]{2,1,0:T(8,128)(2,1)S(1)}, u32[]{:S(2)}, u32[]{:S(2)}) %collective-permute-start.7) | collective-permute-done | bytes 131104 | tf_op jit(solution)/shard_map/ppermute | solution.py:79
  88.6 0.0 collective-permute-done.6
  88.6 0.1 fusion.8
  88.7 1.6 %collective-permute-start.9 = (bf16[4,2,128,256]{3,2,1,0:T(8,128)(2,1)S(1)}, bf16[4,2,128,256]{3,2,1,0:T(8,128)(2,1)S(1)}, u32[]{:S(2)}, u32[]{:S(2)}) collective-permute-start(bf16[4,2,128,256]{3,2,1,0:T(8,128)(2,1)S(1)} %get-tuple-element.16), channel_id=1, source_target_pairs={{0,4},{1,3},{2,6},{3,1},{4,0},{5,7},{6,2},{7,5},{8,12},{9,11},{10,... | collective-permute-start | bytes 1572872 | tf_op jit(solution)/shard_map/ppermute | solution.py:79
  90.2 7.7 %collective-permute-done.9 = bf16[4,2,128,256]{3,2,1,0:T(8,128)(2,1)S(1)} collective-permute-done((bf16[4,2,128,256]{3,2,1,0:T(8,128)(2,1)S(1)}, bf16[4,2,128,256]{3,2,1,0:T(8,128)(2,1)S(1)}, u32[]{:S(2)}, u32[]{:S(2)}) %collective-permute-start.9) | collective-permute-done | bytes 524320 | tf_op jit(solution)/shard_map/ppermute | solution.py:79
  97.9 0.1 fusion.7
  98.0 1.6 %collective-permute-start.10 = (bf16[2,4,2,128,256]{4,3,2,1,0:T(8,128)(2,1)S(1)}, bf16[2,4,2,128,256]{4,3,2,1,0:T(8,128)(2,1)S(1)}, u32[]{:S(2)}, u32[]{:S(2)}) collective-permute-start(bf16[2,4,2,128,256]{4,3,2,1,0:T(8,128)(2,1)S(1)} %get-tuple-element.14), channel_id=1, source_target_pairs={{0,2},{1,5},{2,0},{3,7},{4,6},{5,1},{6,4},{7,3},{8,10},{9,13},{10,... | collective-permute-start | bytes 3145736 | tf_op jit(solution)/shard_map/ppermute | solution.py:79
  99.6 13.3 %collective-permute-done.10 = bf16[2,4,2,128,256]{4,3,2,1,0:T(8,128)(2,1)S(1)} collective-permute-done((bf16[2,4,2,128,256]{4,3,2,1,0:T(8,128)(2,1)S(1)}, bf16[2,4,2,128,256]{4,3,2,1,0:T(8,128)(2,1)S(1)}, u32[]{:S(2)}, u32[]{:S(2)}) %collective-permute-start.10) | collective-permute-done | bytes 1048608 | tf_op jit(solution)/shard_map/ppermute | solution.py:79
  112.9 0.2 pad_maximum_fusion.refs_0_
  113.1 0.0 copy-start
  113.1 0.1 collective-permute-start.11
  113.2 0.7 pad_add_fusion.place
  113.9 3.5 %collective-permute-done.11.refs_1_ = bf16[2,2,4,2,128,256]{5,4,3,2,1,0:T(8,128)(2,1)S(1)} collective-permute-done((bf16[2,2,4,2,128,256]{5,4,3,2,1,0:T(8,128)(2,1)S(1)}, bf16[2,2,4,2,128,256]{5,4,3,2,1,0:T(8,128)(2,1)S(1)}, u32[]{:S(2)}, u32[]{:S(2)}) %collective-permute-start.11) | collective-permute-done | bytes 2097184 | tf_op jit(solution)/shard_map/ppermute | solution.py:79
  117.3 0.0 copy-start.2
  117.3 0.0 copy-done
  117.3 1.3 copy-done.2
  118.6 24.2 %adjoint.1 = bf16[2,2,2,128,2048]{4,3,2,1,0:T(8,128)(2,1)} custom-call(s32[4]{0:T(128)} %pad_add_fusion.place, bf16[2,2,4,2,128,256]{5,4,3,2,1,0:T(8,128)(2,1)} %copy-done, bf16[2,2,4,2,128,256]{5,4,3,2,1,0:T(8,128)(2,1)} %copy-done.2, bf16[2048,2048]{1,0:T(8,128)(2,1)} %get-tuple-element.11.refs_2_, bf16[2048,2048]{1,0:T(8,128)(2,1)} %get-tuple-element.12.refs_3_), custom_call_target="tpu_custom_call" | custom-call | tf_op jit(solution)/shard_map/adjoint/pallas_call | solution.py:198
  (3 shorter events, 0.1 us)
Async XLA Ops:
  25.7 4.5 %collective-permute-start = (bf16[4,4,2,128,256]{4,3,2,1,0:T(8,128)(2,1)}, bf16[4,4,2,128,256]{4,3,2,1,0:T(8,128)(2,1)S(1)}, u32[]{:S(2)}, u32[]{:S(2)}) collective-permute-start(bf16[4,4,2,128,256]{4,3,2,1,0:T(8,128)(2,1)} %get-tuple-element.10), channel_id=1, source_target_pairs={{0,1},{1,0},{2,3},{3,2},{4,5},{5,4},{6,7},{7,6},{8,9},{9,8},{10,11... | collective-permute-start | bytes 6291464 | tf_op jit(solution)/shard_map/ppermute | solution.py:79
  30.2 1.3 copy-start.1
  34.6 15.8 %collective-permute-start.1 = (bf16[2,4,2,128,256]{4,3,2,1,0:T(8,128)(2,1)S(1)}, bf16[2,4,2,128,256]{4,3,2,1,0:T(8,128)(2,1)}, u32[]{:S(2)}, u32[]{:S(2)}) collective-permute-start(bf16[2,4,2,128,256]{4,3,2,1,0:T(8,128)(2,1)S(1)} %dynamic-slice_bitcast_fusion), channel_id=1, source_target_pairs={{0,2},{1,5},{2,0},{3,7},{4,6},{5,1},{6,4},{7,3},{8,10},{9,13},{10,... | collective-permute-start | bytes 3145736 | tf_op jit(solution)/shard_map/ppermute | solution.py:79
  52.0 14.7 %copy-start.4 = (f32[128,256]{1,0:T(8,128)S(1)}, f32[128,256]{1,0:T(8,128)}, u32[]{:S(2)}) copy-start(f32[128,256]{1,0:T(8,128)} %param.8) | copy-start | bytes 393220
  52.0 14.7 %copy-start.5 = (s32[128,256]{1,0:T(8,128)S(1)}, s32[128,256]{1,0:T(8,128)}, u32[]{:S(2)}) copy-start(s32[128,256]{1,0:T(8,128)} %param.9) | copy-start | bytes 393220
  52.0 24.2 %copy-start.3 = (f32[2,128,256]{2,1,0:T(8,128)S(1)}, f32[2,128,256]{2,1,0:T(8,128)}, u32[]{:S(2)}) copy-start(f32[2,128,256]{2,1,0:T(8,128)} %param.7) | copy-start | bytes 786436
  52.1 9.2 %collective-permute-start.2 = (bf16[4,2,128,256]{3,2,1,0:T(8,128)(2,1)S(1)}, bf16[4,2,128,256]{3,2,1,0:T(8,128)(2,1)S(1)}, u32[]{:S(2)}, u32[]{:S(2)}) collective-permute-start(bf16[4,2,128,256]{3,2,1,0:T(8,128)(2,1)S(1)} %dynamic-slice_bitcast_fusion.1), channel_id=1, source_target_pairs={{0,4},{1,3},{2,6},{3,1},{4,0},{5,7},{6,2},{7,5},{8,12},{9,11},{10,... | collective-permute-start | bytes 1572872 | tf_op jit(solution)/shard_map/ppermute | solution.py:79
  61.5 8.6 %collective-permute-start.3 = (bf16[2,128,256]{2,1,0:T(8,128)(2,1)S(1)}, bf16[2,128,256]{2,1,0:T(8,128)(2,1)S(1)}, u32[]{:S(2)}, u32[]{:S(2)}) collective-permute-start(bf16[2,128,256]{2,1,0:T(8,128)(2,1)S(1)} %get-tuple-element.17), channel_id=1, source_target_pairs={{0,8},{1,9},{2,10},{3,11},{4,12},{5,13},{6,14},{7,15},{8,16},{9,17... | collective-permute-start | bytes 393224 | tf_op jit(solution)/shard_map/ppermute | solution.py:79
  63.6 6.5 %collective-permute-start.5 = (bf16[2,128,256]{2,1,0:T(8,128)(2,1)S(1)}, bf16[2,128,256]{2,1,0:T(8,128)(2,1)S(1)}, u32[]{:S(2)}, u32[]{:S(2)}) collective-permute-start(bf16[2,128,256]{2,1,0:T(8,128)(2,1)S(1)} %get-tuple-element.18), channel_id=1, source_target_pairs={{0,24},{1,25},{2,26},{3,27},{4,28},{5,29},{6,30},{7,31},{8,0},{9,1... | collective-permute-start | bytes 393224 | tf_op jit(solution)/shard_map/ppermute | solution.py:79
  65.7 10.4 %collective-permute-start.4 = (bf16[2,128,256]{2,1,0:T(8,128)(2,1)S(1)}, bf16[2,128,256]{2,1,0:T(8,128)(2,1)S(1)}, u32[]{:S(2)}, u32[]{:S(2)}) collective-permute-start(bf16[2,128,256]{2,1,0:T(8,128)(2,1)S(1)} %get-tuple-element.19), channel_id=1, source_target_pairs={{0,16},{1,17},{2,18},{3,19},{4,20},{5,21},{6,22},{7,23},{8,24},{9,... | collective-permute-start | bytes 393224 | tf_op jit(solution)/shard_map/ppermute | solution.py:79
  76.3 6.2 %collective-permute-start.8 = (bf16[2,128,256]{2,1,0:T(8,128)(2,1)S(1)}, bf16[2,128,256]{2,1,0:T(8,128)(2,1)S(1)}, u32[]{:S(2)}, u32[]{:S(2)}) collective-permute-start(bf16[2,128,256]{2,1,0:T(8,128)(2,1)S(1)} %fusion.6), channel_id=1, source_target_pairs={{0,24},{1,25},{2,26},{3,27},{4,28},{5,29},{6,30},{7,31},{8,0},{9,1... | collective-permute-start | bytes 393224 | tf_op jit(solution)/shard_map/ppermute | solution.py:79
  78.5 10.0 %collective-permute-start.7 = (bf16[2,128,256]{2,1,0:T(8,128)(2,1)S(1)}, bf16[2,128,256]{2,1,0:T(8,128)(2,1)S(1)}, u32[]{:S(2)}, u32[]{:S(2)}) collective-permute-start(bf16[2,128,256]{2,1,0:T(8,128)(2,1)S(1)} %fusion.6), channel_id=1, source_target_pairs={{0,16},{1,17},{2,18},{3,19},{4,20},{5,21},{6,22},{7,23},{8,24},{9,... | collective-permute-start | bytes 393224 | tf_op jit(solution)/shard_map/ppermute | solution.py:79
  78.5 10.0 %collective-permute-start.6 = (bf16[2,128,256]{2,1,0:T(8,128)(2,1)S(1)}, bf16[2,128,256]{2,1,0:T(8,128)(2,1)S(1)}, u32[]{:S(2)}, u32[]{:S(2)}) collective-permute-start(bf16[2,128,256]{2,1,0:T(8,128)(2,1)S(1)} %fusion.6), channel_id=1, source_target_pairs={{0,8},{1,9},{2,10},{3,11},{4,12},{5,13},{6,14},{7,15},{8,16},{9,17... | collective-permute-start | bytes 393224 | tf_op jit(solution)/shard_map/ppermute | solution.py:79
  88.7 9.2 %collective-permute-start.9 = (bf16[4,2,128,256]{3,2,1,0:T(8,128)(2,1)S(1)}, bf16[4,2,128,256]{3,2,1,0:T(8,128)(2,1)S(1)}, u32[]{:S(2)}, u32[]{:S(2)}) collective-permute-start(bf16[4,2,128,256]{3,2,1,0:T(8,128)(2,1)S(1)} %get-tuple-element.16), channel_id=1, source_target_pairs={{0,4},{1,3},{2,6},{3,1},{4,0},{5,7},{6,2},{7,5},{8,12},{9,11},{10,... | collective-permute-start | bytes 1572872 | tf_op jit(solution)/shard_map/ppermute | solution.py:79
  98.0 14.9 %collective-permute-start.10 = (bf16[2,4,2,128,256]{4,3,2,1,0:T(8,128)(2,1)S(1)}, bf16[2,4,2,128,256]{4,3,2,1,0:T(8,128)(2,1)S(1)}, u32[]{:S(2)}, u32[]{:S(2)}) collective-permute-start(bf16[2,4,2,128,256]{4,3,2,1,0:T(8,128)(2,1)S(1)} %get-tuple-element.14), channel_id=1, source_target_pairs={{0,2},{1,5},{2,0},{3,7},{4,6},{5,1},{6,4},{7,3},{8,10},{9,13},{10,... | collective-permute-start | bytes 3145736 | tf_op jit(solution)/shard_map/ppermute | solution.py:79
  113.1 4.2 %copy-start = (bf16[2,2,4,2,128,256]{5,4,3,2,1,0:T(8,128)(2,1)}, bf16[2,2,4,2,128,256]{5,4,3,2,1,0:T(8,128)(2,1)S(1)}, u32[]{:S(2)}) copy-start(bf16[2,2,4,2,128,256]{5,4,3,2,1,0:T(8,128)(2,1)S(1)} %pad_maximum_fusion.refs_0_) | copy-start | bytes 6291460
  113.1 4.2 %collective-permute-start.11 = (bf16[2,2,4,2,128,256]{5,4,3,2,1,0:T(8,128)(2,1)S(1)}, bf16[2,2,4,2,128,256]{5,4,3,2,1,0:T(8,128)(2,1)S(1)}, u32[]{:S(2)}, u32[]{:S(2)}) collective-permute-start(bf16[2,2,4,2,128,256]{5,4,3,2,1,0:T(8,128)(2,1)S(1)} %pad_maximum_fusion.refs_0_), channel_id=1, source_target_pairs={{0,1},{1,0},{2,3},{3,2},{4,5},{5,4},{6,7},{7,6},{8,9},{9,8},{10,11... | collective-permute-start | bytes 6291464 | tf_op jit(solution)/shard_map/ppermute | solution.py:79
  117.3 1.3 copy-start.2

commit v2 on v1

--- a/solution.py
+++ b/solution.py
@@ -7,6 +7,7 @@
 from jax.experimental import pallas as pl
 from jax.experimental.pallas import tpu as pltpu
 from jax.sharding import PartitionSpec as P
+
 
 NG = 32768
 FROWS = 4
@@ -45,6 +46,7 @@
         self.near = 2 if self.facets % 2 == 0 else 1
         self.far = self.facets // self.near
         self.mixed = self.high == self.near and self.cores == 2
+        self.fast = self.mixed and self.high == 2
 
     def place(self):
         strip = lax.axis_index("strip")
@@ -229,9 +231,9 @@
     return jnp.stack([value] + [lay.send(value, stage, shift) for shift in range(1, size)])
 
 
-def on_device(lay, facets, offsets, visibilities, weights, mask):
+def in_stages(lay, facets, offsets, visibilities, weights, mask):
     high, core, far, near = lay.place()
-    _, _, columns, rows = facets.shape
+    _, _, _, rows = facets.shape
     width = visibilities.shape[2]
     own_columns = visibilities.shape[1]
     facet_index = lax.axis_index("facet")
@@ -265,6 +267,340 @@
     return update.reshape(facets.shape)
 
 
+WHOLE = pl.BlockSpec(memory_space=pltpu.VMEM)
+SCALARS = pl.BlockSpec(memory_space=pltpu.SMEM)
+
+
+def table_tile(lay, info, place, cos_ref, sin_ref, near, far, width):
+    rows = cos_ref.shape[1]
+    cells = lay.facets * width // info_offsets(info)
+    digit = place[3] if near == 1 else 1 - place[3]
+    coarse_rows = info[0] + FINE * lax.broadcasted_iota(jnp.int32, (rows // FINE, 1), 0)
+    coarse_rows = coarse_rows & (NG - 1)
+    fine_rows = lax.broadcasted_iota(jnp.int32, (FINE, 1), 0)
+    start = (far * lay.near + digit) * width
+    frequency = info[2 + start // cells] + start % cells + lax.broadcasted_iota(jnp.int32, (1, width), 1)
+    frequency = frequency & (NG - 1)
+    coarse_cos, coarse_sin = unit_circle(coarse_rows * frequency)
+    fine_cos, fine_sin = unit_circle(fine_rows * frequency)
+    spot = slice(far * width, (far + 1) * width)
+    for block in range(rows // FINE):
+        c = coarse_cos[block : block + 1]
+        s = coarse_sin[block : block + 1]
+        place_rows = slice(block * FINE, (block + 1) * FINE)
+        cos_ref[near, place_rows, spot] = (c * fine_cos - s * fine_sin).astype(bf16)
+        sin_ref[near, place_rows, spot] = (s * fine_cos + c * fine_sin).astype(bf16)
+
+
+LIMIT = 8 << 20
+
+
+def turned(values, cosine, sine, scale):
+    half = values.shape[0] // 2
+    with_cos = jnp.dot(values, cosine, preferred_element_type=f32)
+    with_sin = jnp.dot(values, sine, preferred_element_type=f32)
+    real = ((with_cos[:half] + with_sin[half:]) * scale).astype(bf16)
+    imag = ((with_cos[half:] - with_sin[:half]) * scale).astype(bf16)
+    return real, imag
+
+
+def store_both(outs, far, real, imag):
+    depth = real.shape[0] // 2
+    for i, out in enumerate(outs):
+        out[far, 0] = real[i * depth : (i + 1) * depth]
+        out[far, 1] = imag[i * depth : (i + 1) * depth]
+
+
+def opening_kernel(lay, scale, info, place, data, away, keep, cos_ref, sin_ref):
+    width = away.shape[-1]
+    cores = (1 - place[1], place[1])
+    values = jnp.concatenate([data[part, 0, core] for part in range(2) for core in cores], axis=0)
+    fill = functools.partial(table_tile, lay, info, place, cos_ref, sin_ref, width=width)
+    fill(0, 0)
+    for far in range(lay.far):
+        spot = slice(far * width, (far + 1) * width)
+        store_both((away, keep), far, *turned(values, cos_ref[0, :, spot], sin_ref[0, :, spot], scale))
+        if far + 1 < lay.far:
+            fill(0, far + 1)
+        fill(1, far)
+
+
+def opening(lay, scale, info, place, data, width):
+    depth, rows = data.shape[-2:]
+    total = lay.far * width
+    half = jax.ShapeDtypeStruct((lay.far, 2, depth, width), bf16)
+    return pl.pallas_call(
+        functools.partial(opening_kernel, lay, scale),
+        out_shape=[half] * 2 + [pltpu.VMEM((2, rows, total), bf16)] * 2,
+        grid_spec=pltpu.PrefetchScalarGridSpec(
+            num_scalar_prefetch=2,
+            grid=(1,),
+            in_specs=[pl.BlockSpec((2, 1, 2, depth, rows), lambda t, info, place: (0, 1 - place[0], 0, 0, 0))],
+            out_specs=[WHOLE] * 4,
+        ),
+        compiler_params=pltpu.CompilerParams(vmem_limit_bytes=LIMIT),
+        name="opening",
+    )(info, place, data)
+
+
+def closing_kernel(lay, scale, place, data, cos_ref, sin_ref, away, keep):
+    width = away.shape[-1]
+
+    def tile(far, carry):
+        spot = pl.ds(far * width, width)
+        cores = (1 - place[1], place[1])
+        values = jnp.concatenate([data[part, place[0], core] for part in range(2) for core in cores], axis=0)
+        store_both((away, keep), far, *turned(values, cos_ref[1, :, spot], sin_ref[1, :, spot], scale))
+        return carry
+
+    lax.fori_loop(0, lay.far, tile, 0, unroll=True)
+
+
+def side_kernel(lay, scale, first, other, place, data, cos_ref, sin_ref, out):
+    width = out.shape[-1]
+    core = 1 - place[1] if other else place[1]
+    mine = jnp.where(core == 0, first, 1 - first)
+    digit = jnp.where(mine == 1, place[0], 1 - place[0])
+    near = 1 - mine
+
+    def tile(far, carry):
+        spot = pl.ds(far * width, width)
+        values = jnp.concatenate([data[part, digit, core] for part in range(2)], axis=0)
+        real, imag = turned(values, cos_ref[near, :, spot], sin_ref[near, :, spot], scale)
+        out[far, 0] = real
+        out[far, 1] = imag
+        return carry
+
+    lax.fori_loop(0, lay.far, tile, 0, unroll=True)
+
+
+def piece(lay, kernel, count, place, data, tables, width):
+    depth = data.shape[-2]
+    return pl.pallas_call(
+        kernel,
+        out_shape=[jax.ShapeDtypeStruct((lay.far, 2, depth, width), bf16)] * count,
+        in_specs=[SCALARS] + [WHOLE] * 3,
+        out_specs=[WHOLE] * count,
+        compiler_params=pltpu.CompilerParams(vmem_limit_bytes=LIMIT),
+        name="piece",
+    )(place, data, *tables)
+
+
+def blocks_kernel(lay, place, held, *refs):
+    parts = refs[: -lay.far]
+    for shift, out in enumerate(refs[-lay.far :]):
+        far = lax.rem(place[2] + shift, lay.far)
+        out[...] = total_of(held[far], *[part[far] for part in parts]).astype(out.dtype)
+
+
+def blocks(lay, place, held, *parts):
+    shape = held.shape[1:]
+    types = [f32] + [bf16] * (lay.far - 1)
+    return pl.pallas_call(
+        functools.partial(blocks_kernel, lay),
+        out_shape=[jax.ShapeDtypeStruct(shape, kind) for kind in types],
+        in_specs=[SCALARS] + [WHOLE] * (1 + len(parts)),
+        out_specs=[WHOLE] * lay.far,
+        compiler_params=pltpu.CompilerParams(vmem_limit_bytes=LIMIT),
+        name="blocks",
+    )(place, held, *parts)
+
+
+def fill_left(lay, place, left, own, other):
+    width = own.shape[-1]
+    for i, source in enumerate((own, other)):
+        core = place[1] if i == 0 else 1 - place[1]
+        for third in range(lay.far):
+            far = lax.rem(place[2] - third + lay.far, lay.far)
+            spot = pl.ds(pl.multiple_of(far * width, width), width)
+            for part in range(2):
+                left[core, part, :, spot] = source[third, part]
+
+
+def back(values, cos_ref, sin_ref, near, spot):
+    contract = (((1,), (1,)), ((), ()))
+    with_cos = lax.dot_general(values, cos_ref[near, spot], contract, preferred_element_type=f32)
+    with_sin = lax.dot_general(values, sin_ref[near, spot], contract, preferred_element_type=f32)
+    half = values.shape[0] // 2
+    return with_cos[:half] - with_sin[half:], with_cos[half:] + with_sin[:half]
+
+
+def rows_of(left, cores):
+    values = [left[core, part] for part in range(2) for core in cores]
+    return jnp.concatenate(values, axis=0)
+
+
+def begin_kernel(lay, step, place, own, other, cos_ref, sin_ref, total, left):
+    fill_left(lay, place, left, own, other)
+    depth = left.shape[2]
+
+    def tile(t, carry):
+        spot = pl.ds(t * step, step)
+        real, imag = back(rows_of(left, (0, 1)), cos_ref, sin_ref, 1, spot)
+        for core in range(2):
+            total[core, 0, :, spot] = real[core * depth : (core + 1) * depth]
+            total[core, 1, :, spot] = imag[core * depth : (core + 1) * depth]
+        return carry
+
+    lax.fori_loop(0, cos_ref.shape[1] // step, tile, 0, unroll=True)
+
+
+def begin(lay, pair, tables, place):
+    _, rows, total = tables[0].shape
+    depth = pair[0].shape[-2]
+    return pl.pallas_call(
+        functools.partial(begin_kernel, lay, tile_of(rows)),
+        out_shape=pltpu.VMEM((2, 2, depth, rows), f32),
+        in_specs=[SCALARS] + [WHOLE] * 4,
+        out_specs=WHOLE,
+        scratch_shapes=[pltpu.VMEM((2, 2, depth, total), bf16)],
+        compiler_params=pltpu.CompilerParams(vmem_limit_bytes=LIMIT),
+        name="begin",
+    )(place, *pair, *tables)
+
+
+def tile_of(rows):
+    return 512 if rows % 512 == 0 else rows
+
+
+def middle_kernel(lay, scale, ending, place, own, other, cos_ref, sin_ref, total, *refs):
+    *_, out, begun, left, ready, sent = refs
+    fill_left(lay, place, left, own, other)
+    slots, *_, step = ready.shape
+    copies = []
+    for t in range(slots):
+        spot = pl.ds(t * step, step)
+        real, imag = back(rows_of(left, (ending,)), cos_ref, sin_ref, 0, spot)
+        ready[t, 0, 0] = ((total[ending, 0, :, spot] + real) * scale).astype(bf16)
+        ready[t, 1, 0] = ((total[ending, 1, :, spot] + imag) * scale).astype(bf16)
+        target = out.at[:, place[0], ending : ending + 1, :, spot]
+        copies.append(pltpu.make_async_copy(ready.at[t], target, sent.at[t]))
+        copies[-1].start()
+        real, imag = back(rows_of(left, (1 - ending,)), cos_ref, sin_ref, 1, spot)
+        begun[0, :, spot] = real
+        begun[1, :, spot] = imag
+    for copy in copies:
+        copy.wait()
+
+
+def finish_kernel(lay, scale, place, own, other, cos_ref, sin_ref, *refs):
+    *totals, _, out, left, ready, sent = refs
+    fill_left(lay, place, left, own, other)
+    depth = left.shape[2]
+    slots, *_, step = ready.shape
+    copies = []
+    for t in range(slots):
+        spot = pl.ds(t * step, step)
+        real, imag = back(rows_of(left, (0, 1)), cos_ref, sin_ref, 0, spot)
+        for core, total in enumerate(totals):
+            block = slice(core * depth, (core + 1) * depth)
+            ready[t, 0, core] = ((total[0, :, spot] + real[block]) * scale).astype(bf16)
+            ready[t, 1, core] = ((total[1, :, spot] + imag[block]) * scale).astype(bf16)
+        target = out.at[:, 1 - place[0], :, :, spot]
+        copies.append(pltpu.make_async_copy(ready.at[t], target, sent.at[t]))
+        copies[-1].start()
+    for copy in copies:
+        copy.wait()
+
+
+def written(lay, kernel, place, operands, earlier, cores, begun):
+    _, rows, cells = operands[2].shape
+    depth = operands[0].shape[-2]
+    step = tile_of(rows)
+    specs = [SCALARS] + [WHOLE] * len(operands)
+    if earlier is not None:
+        operands = [*operands, earlier]
+        specs.append(pl.BlockSpec(memory_space=pl.ANY))
+    slots = rows // step
+    return pl.pallas_call(
+        kernel,
+        out_shape=[jax.ShapeDtypeStruct((2, lay.high, 2, depth, rows), bf16)]
+        + [pltpu.VMEM((2, depth, rows), f32)] * begun,
+        in_specs=specs,
+        out_specs=[pl.BlockSpec(memory_space=pl.ANY)] + [WHOLE] * begun,
+        scratch_shapes=[
+            pltpu.VMEM((2, 2, depth, cells), bf16),
+            pltpu.VMEM((slots, 2, cores, depth, step), bf16),
+            pltpu.SemaphoreType.DMA((slots,)),
+        ],
+        input_output_aliases={} if earlier is None else {len(operands): 0},
+        compiler_params=pltpu.CompilerParams(vmem_limit_bytes=LIMIT),
+    )(place, *operands)
+
+
+def middle(lay, pair, tables, total, place, ending, scale, earlier=None):
+    return written(
+        lay, functools.partial(middle_kernel, lay, scale, ending), place, [*pair, *tables, total], earlier, 1, 1
+    )
+
+
+def finish(lay, pair, tables, totals, place, scale, earlier):
+    return written(
+        lay, functools.partial(finish_kernel, lay, scale), place, [*pair, *tables, *totals], earlier, 2, 0
+    )[0]
+
+
+def in_pieces(lay, facets, offsets, visibilities, weights, mask):
+    high, core, far, near = lay.place()
+    _, _, _, rows = facets.shape
+    _, depth, width = visibilities.shape
+    facet_index = lax.axis_index("facet")
+    all_rows = rows * lay.strips
+    base = lax.axis_index("strip") * rows + facet_index % FROWS * all_rows + NG // 2
+    info = jnp.concatenate([jnp.stack([base, core]).astype(jnp.int32), offsets])
+    place = jnp.stack([high, core, far, near]).astype(jnp.int32)
+    scale = 1.0 / math.sqrt(all_rows)
+    data = facets.reshape(2, lay.high, lay.cores, depth, rows)
+
+    def sent(stage, *values):
+        return lay.send(values[0] if len(values) == 1 else total_of(*values).astype(bf16), stage, 1)
+
+    def side(first, other):
+        return piece(lay, functools.partial(side_kernel, lay, scale, first, other), 1, place, data, tables, width)[0]
+
+    away, keep, *tables = opening(lay, scale, info, place, data, width)
+    cross = sent("core", away)
+    away = side(0, True)
+    first_a = sent("first", keep, cross)
+    cross = sent("core", away)
+    keep = side(0, False)
+    first_b = sent("first", keep, cross)
+    away = side(1, True)
+    cross = sent("core", away)
+    keep = side(1, False)
+    second = sent("second", keep, cross, first_a)
+    away, keep = piece(lay, functools.partial(closing_kernel, lay, scale), 2, place, data, tables, width)
+    cross = sent("core", away)
+    own, *others = blocks(lay, place, keep, cross, first_b, second)
+    model = total_of(own, *[lay.send(value, "far", 1 + i) for i, value in enumerate(others)])
+
+    factor = weights * mask.astype(f32)
+    residual = (factor[None] * (visibilities - model)).astype(bf16)
+
+    def paired(value):
+        return [value, sent("core", value)]
+
+    corner = gather_stage(lay, residual, "far", lay.far)
+    over_second = sent("second", corner)
+    corners = paired(corner)
+    total = begin(lay, corners, tables, place)
+    over_first = sent("first", corner)
+    over_both = sent("first", over_second)
+    seconds = paired(over_second)
+    update, begun_one = middle(lay, seconds, tables, total, place, 0, scale)
+    firsts = paired(over_first)
+    update, begun_zero = middle(lay, firsts, tables, total, place, 1, scale, update)
+    boths = paired(over_both)
+    update = finish(lay, boths, tables, (begun_zero, begun_one), place, scale, update)
+    return update.reshape(facets.shape)
+
+
+def on_device(lay, *arrays):
+    if lay.fast:
+        return in_pieces(lay, *arrays)
+    return in_stages(lay, *arrays)
+
+
 def solution(mesh):
     placed = (
         P("facet", None, None, "strip"),
@@ -273,8 +609,9 @@
         P("strip", "facet"),
         P("strip", "facet"),
     )
+    lay = Layout(mesh)
     return jax.shard_map(
-        functools.partial(on_device, Layout(mesh)),
+        functools.partial(on_device, lay),
         mesh=mesh,
         in_specs=placed,
         out_specs=P("facet", None, None, "strip"),

time: 143 us -> 125 us (0.87)
  waiting for transfers between devices: 67.4 us -> 48.1 us
  other arithmetic: 7.12 us -> 1.49 us
  starting transfers between devices: 16.8 us -> 20.8 us
  Pallas kernels: 48.6 us -> 50.5 us
    ppermute x12 -> x20, waiting for transfers between devices: 67.4 us -> 48.1 us  [send(): return lax.ppermute(value, AXES, self.along(stage, shift))]
    convert_element_type x4, other arithmetic: 4.74 us -> 0.59 us  [the longest x3 0.5 us: sent(): total_of(*values).astype(bf16)]
    ppermute x12 -> x20, starting transfers between devices: 16.8 us -> 20.8 us  [send(): return lax.ppermute(value, AXES, self.along(stage, shift))]
    pallas_call x2 -> x11, Pallas kernels: 48.6 us -> 50.5 us  [the longest x3 19 us: written(): pl.pallas_call(kernel, out_shape=[jax.ShapeDtypeStruct((2, lay.high, 2, d...]
  transfers between devices with their start and end apart: 12 -> 20, of which waited for: 10 -> 8; matrix products, arithmetic and copies ran while one was open for 0% -> 0% of each run, Pallas kernels for 0% -> 28%
where the time goes in v2:
time: 125 us; the launch traced here: 123 us
  Pallas kernels  50.5 us (40%)
  waiting for transfers between devices  48.1 us (38%)
  starting transfers between devices  20.8 us (17%)
  local copies, waits for them, and re-layouts  2.21 us (2%)
  other arithmetic  1.49 us (1%)
    ppermute x20, waiting for transfers between devices, send(): return lax.ppermute(value, AXES, self.along(stage, shift))  48.1 us
    ppermute x20, starting transfers between devices, send(): return lax.ppermute(value, AXES, self.along(stage, shift))  20.8 us
    pallas_call x3, Pallas kernels, written(): pl.pallas_call(kernel, out_shape=[jax.ShapeDtypeStruct((2, lay.high, 2, d...  19 us
    pallas_call x5, Pallas kernels, piece(): pl.pallas_call(kernel, out_shape=[jax.ShapeDtypeStruct((lay.far, 2, depth...  17.1 us
    pallas_call x1, Pallas kernels, opening(): pl.pallas_call(functools.partial(opening_kernel, lay, scale), out_shape=[...  8.37 us
    pallas_call x1, Pallas kernels, begin(): pl.pallas_call(functools.partial(begin_kernel, lay, tile_of(rows)), out_s...  5.15 us
  transfers between devices with their start and end apart: 20, of which 8 were waited for; matrix products, arithmetic and copies ran while one was open for 0% of the time, Pallas kernels for 28%

profile of v2, /device:TPU:0, one launch (start us, length us, event | category | flops | bytes accessed | tf_op | source)
XLA Modules:
  0.0 123.4 jit_solution(8219823693357136870)
XLA Ops:
  0.0 0.7 pad_add_fusion.1.info
  0.7 0.1 pad_add_fusion.place
  0.8 2.2 %copy-done = bf16[1,2,512,2048]{3,2,1,0:T(8,128)(2,1)S(1)} copy-done((bf16[1,2,512,2048]{3,2,1,0:T(8,128)(2,1)S(1)}, bf16[1,2,512,2048]{3,2,1,0:T(8,128)(2,1)}, u32[]{:S(2)}) %copy-start) | copy-done | bytes 4194328
  3.0 8.4 %opening.1 = (bf16[4,2,128,256]{3,2,1,0:T(8,128)(2,1)S(1)}, bf16[4,2,128,256]{3,2,1,0:T(8,128)(2,1)S(1)}, bf16[2,2048,1024]{2,1,0:T(8,128)(2,1)S(1)}, bf16[2,2048,1024]{2,1,0:T(8,128)(2,1)S(1)}) custom-call(s32[6]{0:T(128)S(1)} %pad_add_fusion.1.info, s32[4]{0:T(128)S(1)} %pad_add_fusion.place, bf16[2,2,2,128,2048]{4,3,2,1,0:T(8,128)(2,1)S(1)} %bitcast.11), custom_call_target="tpu_custom_call" | custom-call | tf_op jit(solution)/shard_map/opening/pallas_call | solution.py:332
  11.4 0.6 collective-permute-start.4
  11.9 3.0 %piece.9 = bf16[4,2,128,256]{3,2,1,0:T(8,128)(2,1)S(1)} custom-call(s32[4]{0:T(128)S(1)} %pad_add_fusion.place, bf16[2,2,2,128,2048]{4,3,2,1,0:T(8,128)(2,1)S(1)} %bitcast.12, bf16[2,2048,1024]{2,1,0:T(8,128)(2,1)S(1)} %get-tuple-element.19.cos_ref, bf16[2,2048,1024]{2,1,0:T(8,128)(2,1)S(1)} %get-tuple-element.20.sin_ref), custom_call_target="tpu_custom_call" | custom-call | tf_op jit(solution)/shard_map/piece/pallas_call | solution.py:379
  14.9 0.1 collective-permute-start.3
  15.0 3.0 %piece.7 = bf16[4,2,128,256]{3,2,1,0:T(8,128)(2,1)S(1)} custom-call(s32[4]{0:T(128)S(1)} %pad_add_fusion.place, bf16[2,2,2,128,2048]{4,3,2,1,0:T(8,128)(2,1)S(1)} %bitcast.13, bf16[2,2048,1024]{2,1,0:T(8,128)(2,1)S(1)} %get-tuple-element.19.cos_ref, bf16[2,2048,1024]{2,1,0:T(8,128)(2,1)S(1)} %get-tuple-element.20.sin_ref), custom_call_target="tpu_custom_call" | custom-call | tf_op jit(solution)/shard_map/piece/pallas_call | solution.py:379
  18.0 0.6 collective-permute-start.1
  18.5 0.1 add_convert_fusion.1
  18.7 2.6 %collective-permute-start.5 = (bf16[4,2,128,256]{3,2,1,0:T(8,128)(2,1)S(1)}, bf16[4,2,128,256]{3,2,1,0:T(8,128)(2,1)S(1)}, u32[]{:S(2)}, u32[]{:S(2)}) collective-permute-start(bf16[4,2,128,256]{3,2,1,0:T(8,128)(2,1)S(1)} %add_convert_fusion.1), channel_id=1, source_target_pairs={{0,2},{1,5},{2,0},{3,7},{4,6},{5,1},{6,4},{7,3},{8,10},{9,13},{10,... | collective-permute-start | bytes 1572872 | tf_op jit(solution)/shard_map/ppermute | solution.py:81
  21.2 5.3 %piece.5 = (bf16[4,2,128,256]{3,2,1,0:T(8,128)(2,1)S(1)}, bf16[4,2,128,256]{3,2,1,0:T(8,128)(2,1)S(1)}) custom-call(s32[4]{0:T(128)S(1)} %pad_add_fusion.place, bf16[2,2,2,128,2048]{4,3,2,1,0:T(8,128)(2,1)S(1)} %bitcast.14, bf16[2,2048,1024]{2,1,0:T(8,128)(2,1)S(1)} %get-tuple-element.19.cos_ref, bf16[2,2048,1024]{2,1,0:T(8,128)(2,1)S(1)} %get-tuple-element.20.sin_ref), custom_call_target="tpu_custom_call" | custom-call | tf_op jit(solution)/shard_map/piece/pallas_call | solution.py:379
  26.5 0.2 collective-permute-start
  26.8 2.9 %piece.8 = bf16[4,2,128,256]{3,2,1,0:T(8,128)(2,1)S(1)} custom-call(s32[4]{0:T(128)S(1)} %pad_add_fusion.place, bf16[2,2,2,128,2048]{4,3,2,1,0:T(8,128)(2,1)S(1)} %bitcast.15, bf16[2,2048,1024]{2,1,0:T(8,128)(2,1)S(1)} %get-tuple-element.19.cos_ref, bf16[2,2048,1024]{2,1,0:T(8,128)(2,1)S(1)} %get-tuple-element.20.sin_ref), custom_call_target="tpu_custom_call" | custom-call | tf_op jit(solution)/shard_map/piece/pallas_call | solution.py:379
  29.7 2.9 %piece.6 = bf16[4,2,128,256]{3,2,1,0:T(8,128)(2,1)S(1)} custom-call(s32[4]{0:T(128)S(1)} %pad_add_fusion.place, bf16[2,2,2,128,2048]{4,3,2,1,0:T(8,128)(2,1)S(1)} %bitcast.16, bf16[2,2048,1024]{2,1,0:T(8,128)(2,1)S(1)} %get-tuple-element.19.cos_ref, bf16[2,2048,1024]{2,1,0:T(8,128)(2,1)S(1)} %get-tuple-element.20.sin_ref), custom_call_target="tpu_custom_call" | custom-call | tf_op jit(solution)/shard_map/piece/pallas_call | solution.py:379
  32.7 0.0 copy-start.3
  32.7 0.0 copy-start.4
  32.7 0.0 copy-start.2
  32.7 0.1 add_convert_fusion.2
  32.9 1.6 %collective-permute-start.2 = (bf16[4,2,128,256]{3,2,1,0:T(8,128)(2,1)S(1)}, bf16[4,2,128,256]{3,2,1,0:T(8,128)(2,1)S(1)}, u32[]{:S(2)}, u32[]{:S(2)}) collective-permute-start(bf16[4,2,128,256]{3,2,1,0:T(8,128)(2,1)S(1)} %add_convert_fusion.2), channel_id=1, source_target_pairs={{0,2},{1,5},{2,0},{3,7},{4,6},{5,1},{6,4},{7,3},{8,10},{9,13},{10,... | collective-permute-start | bytes 1572872 | tf_op jit(solution)/shard_map/ppermute | solution.py:81
  34.5 0.2 add_convert_fusion
  34.7 0.6 collective-permute-start.6
  35.3 11.6 %collective-permute-done.2.refs_1_ = bf16[4,2,128,256]{3,2,1,0:T(8,128)(2,1)S(1)} collective-permute-done((bf16[4,2,128,256]{3,2,1,0:T(8,128)(2,1)S(1)}, bf16[4,2,128,256]{3,2,1,0:T(8,128)(2,1)S(1)}, u32[]{:S(2)}, u32[]{:S(2)}) %collective-permute-start.2) | collective-permute-done | bytes 524320 | tf_op jit(solution)/shard_map/ppermute | solution.py:81
  46.9 0.2 collective-permute-done.6.refs_2_
  47.1 0.8 blocks.1
  47.9 1.6 %collective-permute-start.7 = (bf16[2,128,256]{2,1,0:T(8,128)(2,1)S(1)}, bf16[2,128,256]{2,1,0:T(8,128)(2,1)S(1)}, u32[]{:S(2)}, u32[]{:S(2)}) collective-permute-start(bf16[2,128,256]{2,1,0:T(8,128)(2,1)S(1)} %get-tuple-element.26), channel_id=1, source_target_pairs={{0,8},{1,9},{2,10},{3,11},{4,12},{5,13},{6,14},{7,15},{8,16},{9,17... | collective-permute-start | bytes 393224 | tf_op jit(solution)/shard_map/ppermute | solution.py:81
  49.6 2.6 %collective-permute-start.8 = (bf16[2,128,256]{2,1,0:T(8,128)(2,1)S(1)}, bf16[2,128,256]{2,1,0:T(8,128)(2,1)S(1)}, u32[]{:S(2)}, u32[]{:S(2)}) collective-permute-start(bf16[2,128,256]{2,1,0:T(8,128)(2,1)S(1)} %get-tuple-element.27), channel_id=1, source_target_pairs={{0,16},{1,17},{2,18},{3,19},{4,20},{5,21},{6,22},{7,23},{8,24},{9,... | collective-permute-start | bytes 393224 | tf_op jit(solution)/shard_map/ppermute | solution.py:81
  52.1 1.3 %collective-permute-start.9 = (bf16[2,128,256]{2,1,0:T(8,128)(2,1)S(1)}, bf16[2,128,256]{2,1,0:T(8,128)(2,1)S(1)}, u32[]{:S(2)}, u32[]{:S(2)}) collective-permute-start(bf16[2,128,256]{2,1,0:T(8,128)(2,1)S(1)} %get-tuple-element.28), channel_id=1, source_target_pairs={{0,24},{1,25},{2,26},{3,27},{4,28},{5,29},{6,30},{7,31},{8,0},{9,1... | collective-permute-start | bytes 393224 | tf_op jit(solution)/shard_map/ppermute | solution.py:81
  53.5 2.7 %collective-permute-done.7 = bf16[2,128,256]{2,1,0:T(8,128)(2,1)S(1)} collective-permute-done((bf16[2,128,256]{2,1,0:T(8,128)(2,1)S(1)}, bf16[2,128,256]{2,1,0:T(8,128)(2,1)S(1)}, u32[]{:S(2)}, u32[]{:S(2)}) %collective-permute-start.7) | collective-permute-done | bytes 131104 | tf_op jit(solution)/shard_map/ppermute | solution.py:81
  56.2 5.2 %collective-permute-done.8 = bf16[2,128,256]{2,1,0:T(8,128)(2,1)S(1)} collective-permute-done((bf16[2,128,256]{2,1,0:T(8,128)(2,1)S(1)}, bf16[2,128,256]{2,1,0:T(8,128)(2,1)S(1)}, u32[]{:S(2)}, u32[]{:S(2)}) %collective-permute-start.8) | collective-permute-done | bytes 131104 | tf_op jit(solution)/shard_map/ppermute | solution.py:81
  61.4 0.1 multiply_convert_fusion
  61.5 3.4 %collective-permute-start.10 = (bf16[2,128,256]{2,1,0:T(8,128)(2,1)S(1)}, bf16[2,128,256]{2,1,0:T(8,128)(2,1)S(1)}, u32[]{:S(2)}, u32[]{:S(2)}) collective-permute-start(bf16[2,128,256]{2,1,0:T(8,128)(2,1)S(1)} %multiply_convert_fusion), channel_id=1, source_target_pairs={{0,8},{1,9},{2,10},{3,11},{4,12},{5,13},{6,14},{7,15},{8,16},{9,17... | collective-permute-start | bytes 393224 | tf_op jit(solution)/shard_map/ppermute | solution.py:81
  64.8 1.6 %collective-permute-start.11 = (bf16[2,128,256]{2,1,0:T(8,128)(2,1)S(1)}, bf16[2,128,256]{2,1,0:T(8,128)(2,1)S(1)}, u32[]{:S(2)}, u32[]{:S(2)}) collective-permute-start(bf16[2,128,256]{2,1,0:T(8,128)(2,1)S(1)} %multiply_convert_fusion), channel_id=1, source_target_pairs={{0,16},{1,17},{2,18},{3,19},{4,20},{5,21},{6,22},{7,23},{8,24},{9,... | collective-permute-start | bytes 393224 | tf_op jit(solution)/shard_map/ppermute | solution.py:81
  66.5 0.8 collective-permute-start.12
  67.3 3.1 %collective-permute-done.10 = bf16[2,128,256]{2,1,0:T(8,128)(2,1)S(1)} collective-permute-done((bf16[2,128,256]{2,1,0:T(8,128)(2,1)S(1)}, bf16[2,128,256]{2,1,0:T(8,128)(2,1)S(1)}, u32[]{:S(2)}, u32[]{:S(2)}) %collective-permute-start.10) | collective-permute-done | bytes 131104 | tf_op jit(solution)/shard_map/ppermute | solution.py:81
  70.4 4.5 %collective-permute-done.11 = bf16[2,128,256]{2,1,0:T(8,128)(2,1)S(1)} collective-permute-done((bf16[2,128,256]{2,1,0:T(8,128)(2,1)S(1)}, bf16[2,128,256]{2,1,0:T(8,128)(2,1)S(1)}, u32[]{:S(2)}, u32[]{:S(2)}) %collective-permute-start.11) | collective-permute-done | bytes 131104 | tf_op jit(solution)/shard_map/ppermute | solution.py:81
  74.9 0.1 pad_maximum_fusion.own
  75.0 1.3 %collective-permute-start.13 = (bf16[4,2,128,256]{3,2,1,0:T(8,128)(2,1)S(1)}, bf16[4,2,128,256]{3,2,1,0:T(8,128)(2,1)S(1)}, u32[]{:S(2)}, u32[]{:S(2)}) collective-permute-start(bf16[4,2,128,256]{3,2,1,0:T(8,128)(2,1)S(1)} %pad_maximum_fusion.own), channel_id=1, source_target_pairs={{0,4},{1,3},{2,6},{3,1},{4,0},{5,7},{6,2},{7,5},{8,12},{9,11},{10,... | collective-permute-start | bytes 1572872 | tf_op jit(solution)/shard_map/ppermute | solution.py:81
  76.2 0.7 collective-permute-start.16
  77.0 12.8 %collective-permute-done.13.own = bf16[4,2,128,256]{3,2,1,0:T(8,128)(2,1)S(1)} collective-permute-done((bf16[4,2,128,256]{3,2,1,0:T(8,128)(2,1)S(1)}, bf16[4,2,128,256]{3,2,1,0:T(8,128)(2,1)S(1)}, u32[]{:S(2)}, u32[]{:S(2)}) %collective-permute-start.13) | collective-permute-done | bytes 524320 | tf_op jit(solution)/shard_map/ppermute | solution.py:81
  89.8 0.7 collective-permute-start.14
  90.5 0.5 collective-permute-start.19
  91.0 0.0 collective-permute-start.17
  91.0 8.0 %collective-permute-done.14.own = bf16[4,2,128,256]{3,2,1,0:T(8,128)(2,1)S(1)} collective-permute-done((bf16[4,2,128,256]{3,2,1,0:T(8,128)(2,1)S(1)}, bf16[4,2,128,256]{3,2,1,0:T(8,128)(2,1)S(1)}, u32[]{:S(2)}, u32[]{:S(2)}) %collective-permute-start.14) | collective-permute-done | bytes 524320 | tf_op jit(solution)/shard_map/ppermute | solution.py:81
  99.0 5.2 %begin.1.total = f32[2,2,128,2048]{3,2,1,0:T(8,128)S(1)} custom-call(s32[4]{0:T(128)S(1)} %pad_add_fusion.place, bf16[4,2,128,256]{3,2,1,0:T(8,128)(2,1)S(1)} %pad_maximum_fusion.own, bf16[4,2,128,256]{3,2,1,0:T(8,128)(2,1)S(1)} %collective-permute-done.18.other, bf16[2,2048,1024]{2,1,0:T(8,128)(2,1)S(1)} %get-tuple-element.19.cos_ref, ...), custom_call_target="tpu_custom_call" | custom-call | tf_op jit(solution)/shard_map/begin/pallas_call | solution.py:451
  104.2 6.1 %shard_map.55 = (bf16[2,2,2,128,2048]{4,3,2,1,0:T(8,128)(2,1)}, f32[2,128,2048]{2,1,0:T(8,128)S(1)}) custom-call(s32[4]{0:T(128)S(1)} %pad_add_fusion.place, bf16[4,2,128,256]{3,2,1,0:T(8,128)(2,1)S(1)} %collective-permute-done.13.own, bf16[4,2,128,256]{3,2,1,0:T(8,128)(2,1)S(1)} %collective-permute-done.19.other, ...), custom_call_target="tpu_custom_call" | custom-call | tf_op jit(solution)/shard_map/pallas_call | solution.py:515
  110.3 6.1 %shard_map.56 = (bf16[2,2,2,128,2048]{4,3,2,1,0:T(8,128)(2,1)}, f32[2,128,2048]{2,1,0:T(8,128)S(1)}) custom-call(s32[4]{0:T(128)S(1)} %pad_add_fusion.place, bf16[4,2,128,256]{3,2,1,0:T(8,128)(2,1)S(1)} %collective-permute-done.16.own, bf16[4,2,128,256]{3,2,1,0:T(8,128)(2,1)S(1)} %collective-permute-done.17.other, ...), custom_call_target="tpu_custom_call", output_to_operand_aliasing={{0}: (6, {})} | custom-call | tf_op jit(solution)/shard_map/pallas_call | solution.py:515
  116.3 6.9 %shard_map.57 = bf16[2,2,2,128,2048]{4,3,2,1,0:T(8,128)(2,1)} custom-call(s32[4]{0:T(128)S(1)} %pad_add_fusion.place, bf16[4,2,128,256]{3,2,1,0:T(8,128)(2,1)S(1)} %collective-permute-done.14.own, bf16[4,2,128,256]{3,2,1,0:T(8,128)(2,1)S(1)} %collective-permute-done.15.other, ...), custom_call_target="tpu_custom_call", output_to_operand_aliasing={{}: (7, {})} | custom-call | tf_op jit(solution)/shard_map/pallas_call | solution.py:515
  (21 shorter events, 0.1 us)
Async XLA Ops:
  0.8 2.2 %copy-start = (bf16[1,2,512,2048]{3,2,1,0:T(8,128)(2,1)S(1)}, bf16[1,2,512,2048]{3,2,1,0:T(8,128)(2,1)}, u32[]{:S(2)}) copy-start(bf16[1,2,512,2048]{3,2,1,0:T(8,128)(2,1)} %param.5) | copy-start | bytes 12582916
  11.4 7.1 %collective-permute-start.4 = (bf16[4,2,128,256]{3,2,1,0:T(8,128)(2,1)S(1)}, bf16[4,2,128,256]{3,2,1,0:T(8,128)(2,1)S(1)}, u32[]{:S(2)}, u32[]{:S(2)}) collective-permute-start(bf16[4,2,128,256]{3,2,1,0:T(8,128)(2,1)S(1)} %get-tuple-element.24), channel_id=1, source_target_pairs={{0,1},{1,0},{2,3},{3,2},{4,5},{5,4},{6,7},{7,6},{8,9},{9,8},{10,11... | collective-permute-start | bytes 1572872 | tf_op jit(solution)/shard_map/ppermute | solution.py:81
  14.9 19.6 %collective-permute-start.3 = (bf16[4,2,128,256]{3,2,1,0:T(8,128)(2,1)S(1)}, bf16[4,2,128,256]{3,2,1,0:T(8,128)(2,1)S(1)}, u32[]{:S(2)}, u32[]{:S(2)}) collective-permute-start(bf16[4,2,128,256]{3,2,1,0:T(8,128)(2,1)S(1)} %piece.9), channel_id=1, source_target_pairs={{0,1},{1,0},{2,3},{3,2},{4,5},{5,4},{6,7},{7,6},{8,9},{9,8},{10,11... | collective-permute-start | bytes 1572872 | tf_op jit(solution)/shard_map/ppermute | solution.py:81
  15.0 6.3 %copy-start.1 = (bf16[1,2,512,2048]{3,2,1,0:T(8,128)(2,1)S(1)}, bf16[1,2,512,2048]{3,2,1,0:T(8,128)(2,1)}, u32[]{:S(2)}) copy-start(bf16[1,2,512,2048]{3,2,1,0:T(8,128)(2,1)} %param.5) | copy-start | bytes 12582916
  18.0 14.8 %collective-permute-start.1 = (bf16[4,2,128,256]{3,2,1,0:T(8,128)(2,1)S(1)}, bf16[4,2,128,256]{3,2,1,0:T(8,128)(2,1)S(1)}, u32[]{:S(2)}, u32[]{:S(2)}) collective-permute-start(bf16[4,2,128,256]{3,2,1,0:T(8,128)(2,1)S(1)} %piece.7), channel_id=1, source_target_pairs={{0,1},{1,0},{2,3},{3,2},{4,5},{5,4},{6,7},{7,6},{8,9},{9,8},{10,11... | collective-permute-start | bytes 1572872 | tf_op jit(solution)/shard_map/ppermute | solution.py:81
  18.7 15.8 %collective-permute-start.5 = (bf16[4,2,128,256]{3,2,1,0:T(8,128)(2,1)S(1)}, bf16[4,2,128,256]{3,2,1,0:T(8,128)(2,1)S(1)}, u32[]{:S(2)}, u32[]{:S(2)}) collective-permute-start(bf16[4,2,128,256]{3,2,1,0:T(8,128)(2,1)S(1)} %add_convert_fusion.1), channel_id=1, source_target_pairs={{0,2},{1,5},{2,0},{3,7},{4,6},{5,1},{6,4},{7,3},{8,10},{9,13},{10,... | collective-permute-start | bytes 1572872 | tf_op jit(solution)/shard_map/ppermute | solution.py:81
  26.5 8.8 %collective-permute-start = (bf16[4,2,128,256]{3,2,1,0:T(8,128)(2,1)S(1)}, bf16[4,2,128,256]{3,2,1,0:T(8,128)(2,1)S(1)}, u32[]{:S(2)}, u32[]{:S(2)}) collective-permute-start(bf16[4,2,128,256]{3,2,1,0:T(8,128)(2,1)S(1)} %get-tuple-element.22), channel_id=1, source_target_pairs={{0,1},{1,0},{2,3},{3,2},{4,5},{5,4},{6,7},{7,6},{8,9},{9,8},{10,11... | collective-permute-start | bytes 1572872 | tf_op jit(solution)/shard_map/ppermute | solution.py:81
  32.7 20.8 %copy-start.3 = (f32[128,256]{1,0:T(8,128)S(1)}, f32[128,256]{1,0:T(8,128)}, u32[]{:S(2)}) copy-start(f32[128,256]{1,0:T(8,128)} %param.8) | copy-start | bytes 393220
  32.7 20.8 %copy-start.4 = (s32[128,256]{1,0:T(8,128)S(1)}, s32[128,256]{1,0:T(8,128)}, u32[]{:S(2)}) copy-start(s32[128,256]{1,0:T(8,128)} %param.9) | copy-start | bytes 393220
  32.7 28.7 %copy-start.2 = (f32[2,128,256]{2,1,0:T(8,128)S(1)}, f32[2,128,256]{2,1,0:T(8,128)}, u32[]{:S(2)}) copy-start(f32[2,128,256]{2,1,0:T(8,128)} %param.7) | copy-start | bytes 786436
  32.9 14.0 %collective-permute-start.2 = (bf16[4,2,128,256]{3,2,1,0:T(8,128)(2,1)S(1)}, bf16[4,2,128,256]{3,2,1,0:T(8,128)(2,1)S(1)}, u32[]{:S(2)}, u32[]{:S(2)}) collective-permute-start(bf16[4,2,128,256]{3,2,1,0:T(8,128)(2,1)S(1)} %add_convert_fusion.2), channel_id=1, source_target_pairs={{0,2},{1,5},{2,0},{3,7},{4,6},{5,1},{6,4},{7,3},{8,10},{9,13},{10,... | collective-permute-start | bytes 1572872 | tf_op jit(solution)/shard_map/ppermute | solution.py:81
  34.7 12.4 %collective-permute-start.6 = (bf16[4,2,128,256]{3,2,1,0:T(8,128)(2,1)S(1)}, bf16[4,2,128,256]{3,2,1,0:T(8,128)(2,1)S(1)}, u32[]{:S(2)}, u32[]{:S(2)}) collective-permute-start(bf16[4,2,128,256]{3,2,1,0:T(8,128)(2,1)S(1)} %add_convert_fusion), channel_id=1, source_target_pairs={{0,4},{1,3},{2,6},{3,1},{4,0},{5,7},{6,2},{7,5},{8,12},{9,11},{10,... | collective-permute-start | bytes 1572872 | tf_op jit(solution)/shard_map/ppermute | solution.py:81
  47.9 8.3 %collective-permute-start.7 = (bf16[2,128,256]{2,1,0:T(8,128)(2,1)S(1)}, bf16[2,128,256]{2,1,0:T(8,128)(2,1)S(1)}, u32[]{:S(2)}, u32[]{:S(2)}) collective-permute-start(bf16[2,128,256]{2,1,0:T(8,128)(2,1)S(1)} %get-tuple-element.26), channel_id=1, source_target_pairs={{0,8},{1,9},{2,10},{3,11},{4,12},{5,13},{6,14},{7,15},{8,16},{9,17... | collective-permute-start | bytes 393224 | tf_op jit(solution)/shard_map/ppermute | solution.py:81
  49.6 11.8 %collective-permute-start.8 = (bf16[2,128,256]{2,1,0:T(8,128)(2,1)S(1)}, bf16[2,128,256]{2,1,0:T(8,128)(2,1)S(1)}, u32[]{:S(2)}, u32[]{:S(2)}) collective-permute-start(bf16[2,128,256]{2,1,0:T(8,128)(2,1)S(1)} %get-tuple-element.27), channel_id=1, source_target_pairs={{0,16},{1,17},{2,18},{3,19},{4,20},{5,21},{6,22},{7,23},{8,24},{9,... | collective-permute-start | bytes 393224 | tf_op jit(solution)/shard_map/ppermute | solution.py:81
  52.1 9.2 %collective-permute-start.9 = (bf16[2,128,256]{2,1,0:T(8,128)(2,1)S(1)}, bf16[2,128,256]{2,1,0:T(8,128)(2,1)S(1)}, u32[]{:S(2)}, u32[]{:S(2)}) collective-permute-start(bf16[2,128,256]{2,1,0:T(8,128)(2,1)S(1)} %get-tuple-element.28), channel_id=1, source_target_pairs={{0,24},{1,25},{2,26},{3,27},{4,28},{5,29},{6,30},{7,31},{8,0},{9,1... | collective-permute-start | bytes 393224 | tf_op jit(solution)/shard_map/ppermute | solution.py:81
  61.5 8.9 %collective-permute-start.10 = (bf16[2,128,256]{2,1,0:T(8,128)(2,1)S(1)}, bf16[2,128,256]{2,1,0:T(8,128)(2,1)S(1)}, u32[]{:S(2)}, u32[]{:S(2)}) collective-permute-start(bf16[2,128,256]{2,1,0:T(8,128)(2,1)S(1)} %multiply_convert_fusion), channel_id=1, source_target_pairs={{0,8},{1,9},{2,10},{3,11},{4,12},{5,13},{6,14},{7,15},{8,16},{9,17... | collective-permute-start | bytes 393224 | tf_op jit(solution)/shard_map/ppermute | solution.py:81
  64.8 10.0 %collective-permute-start.11 = (bf16[2,128,256]{2,1,0:T(8,128)(2,1)S(1)}, bf16[2,128,256]{2,1,0:T(8,128)(2,1)S(1)}, u32[]{:S(2)}, u32[]{:S(2)}) collective-permute-start(bf16[2,128,256]{2,1,0:T(8,128)(2,1)S(1)} %multiply_convert_fusion), channel_id=1, source_target_pairs={{0,16},{1,17},{2,18},{3,19},{4,20},{5,21},{6,22},{7,23},{8,24},{9,... | collective-permute-start | bytes 393224 | tf_op jit(solution)/shard_map/ppermute | solution.py:81
  66.5 8.4 %collective-permute-start.12 = (bf16[2,128,256]{2,1,0:T(8,128)(2,1)S(1)}, bf16[2,128,256]{2,1,0:T(8,128)(2,1)S(1)}, u32[]{:S(2)}, u32[]{:S(2)}) collective-permute-start(bf16[2,128,256]{2,1,0:T(8,128)(2,1)S(1)} %multiply_convert_fusion), channel_id=1, source_target_pairs={{0,24},{1,25},{2,26},{3,27},{4,28},{5,29},{6,30},{7,31},{8,0},{9,1... | collective-permute-start | bytes 393224 | tf_op jit(solution)/shard_map/ppermute | solution.py:81
  75.0 14.9 %collective-permute-start.13 = (bf16[4,2,128,256]{3,2,1,0:T(8,128)(2,1)S(1)}, bf16[4,2,128,256]{3,2,1,0:T(8,128)(2,1)S(1)}, u32[]{:S(2)}, u32[]{:S(2)}) collective-permute-start(bf16[4,2,128,256]{3,2,1,0:T(8,128)(2,1)S(1)} %pad_maximum_fusion.own), channel_id=1, source_target_pairs={{0,4},{1,3},{2,6},{3,1},{4,0},{5,7},{6,2},{7,5},{8,12},{9,11},{10,... | collective-permute-start | bytes 1572872 | tf_op jit(solution)/shard_map/ppermute | solution.py:81
  76.2 14.8 %collective-permute-start.16 = (bf16[4,2,128,256]{3,2,1,0:T(8,128)(2,1)S(1)}, bf16[4,2,128,256]{3,2,1,0:T(8,128)(2,1)S(1)}, u32[]{:S(2)}, u32[]{:S(2)}) collective-permute-start(bf16[4,2,128,256]{3,2,1,0:T(8,128)(2,1)S(1)} %pad_maximum_fusion.own), channel_id=1, source_target_pairs={{0,2},{1,5},{2,0},{3,7},{4,6},{5,1},{6,4},{7,3},{8,10},{9,13},{10,... | collective-permute-start | bytes 1572872 | tf_op jit(solution)/shard_map/ppermute | solution.py:81
  89.8 9.2 %collective-permute-start.14 = (bf16[4,2,128,256]{3,2,1,0:T(8,128)(2,1)S(1)}, bf16[4,2,128,256]{3,2,1,0:T(8,128)(2,1)S(1)}, u32[]{:S(2)}, u32[]{:S(2)}) collective-permute-start(bf16[4,2,128,256]{3,2,1,0:T(8,128)(2,1)S(1)} %collective-permute-done.13.own), channel_id=1, source_target_pairs={{0,2},{1,5},{2,0},{3,7},{4,6},{5,1},{6,4},{7,3},{8,10},{9,13},{10,... | collective-permute-start | bytes 1572872 | tf_op jit(solution)/shard_map/ppermute | solution.py:81
  90.5 8.5 %collective-permute-start.18 = (bf16[4,2,128,256]{3,2,1,0:T(8,128)(2,1)S(1)}, bf16[4,2,128,256]{3,2,1,0:T(8,128)(2,1)S(1)}, u32[]{:S(2)}, u32[]{:S(2)}) collective-permute-start(bf16[4,2,128,256]{3,2,1,0:T(8,128)(2,1)S(1)} %pad_maximum_fusion.own), channel_id=1, source_target_pairs={{0,1},{1,0},{2,3},{3,2},{4,5},{5,4},{6,7},{7,6},{8,9},{9,8},{10,11... | collective-permute-start | bytes 1572872 | tf_op jit(solution)/shard_map/ppermute | solution.py:81
  90.5 13.6 %collective-permute-start.19 = (bf16[4,2,128,256]{3,2,1,0:T(8,128)(2,1)S(1)}, bf16[4,2,128,256]{3,2,1,0:T(8,128)(2,1)S(1)}, u32[]{:S(2)}, u32[]{:S(2)}) collective-permute-start(bf16[4,2,128,256]{3,2,1,0:T(8,128)(2,1)S(1)} %collective-permute-done.13.own), channel_id=1, source_target_pairs={{0,1},{1,0},{2,3},{3,2},{4,5},{5,4},{6,7},{7,6},{8,9},{9,8},{10,11... | collective-permute-start | bytes 1572872 | tf_op jit(solution)/shard_map/ppermute | solution.py:81
  91.0 19.2 %collective-permute-start.17 = (bf16[4,2,128,256]{3,2,1,0:T(8,128)(2,1)S(1)}, bf16[4,2,128,256]{3,2,1,0:T(8,128)(2,1)S(1)}, u32[]{:S(2)}, u32[]{:S(2)}) collective-permute-start(bf16[4,2,128,256]{3,2,1,0:T(8,128)(2,1)S(1)} %collective-permute-done.16.own), channel_id=1, source_target_pairs={{0,1},{1,0},{2,3},{3,2},{4,5},{5,4},{6,7},{7,6},{8,9},{9,8},{10,11... | collective-permute-start | bytes 1572872 | tf_op jit(solution)/shard_map/ppermute | solution.py:81
  99.0 17.3 %collective-permute-start.15 = (bf16[4,2,128,256]{3,2,1,0:T(8,128)(2,1)S(1)}, bf16[4,2,128,256]{3,2,1,0:T(8,128)(2,1)S(1)}, u32[]{:S(2)}, u32[]{:S(2)}) collective-permute-start(bf16[4,2,128,256]{3,2,1,0:T(8,128)(2,1)S(1)} %collective-permute-done.14.own), channel_id=1, source_target_pairs={{0,1},{1,0},{2,3},{3,2},{4,5},{5,4},{6,7},{7,6},{8,9},{9,8},{10,11... | collective-permute-start | bytes 1572872 | tf_op jit(solution)/shard_map/ppermute | solution.py:81

commit v3 on v2

--- a/solution.py
+++ b/solution.py
@@ -11,7 +11,7 @@
 
 NG = 32768
 FROWS = 4
-FINE = 32
+FINE = 16
 AXES = ("facet", "strip")
 bf16 = jnp.bfloat16
 f32 = jnp.float32
@@ -275,24 +275,33 @@
     rows = cos_ref.shape[1]
     cells = lay.facets * width // info_offsets(info)
     digit = place[3] if near == 1 else 1 - place[3]
-    coarse_rows = info[0] + FINE * lax.broadcasted_iota(jnp.int32, (rows // FINE, 1), 0)
-    coarse_rows = coarse_rows & (NG - 1)
-    fine_rows = lax.broadcasted_iota(jnp.int32, (FINE, 1), 0)
+    blocks = rows // FINE
+    middle = blocks // 2
     start = (far * lay.near + digit) * width
     frequency = info[2 + start // cells] + start % cells + lax.broadcasted_iota(jnp.int32, (1, width), 1)
     frequency = frequency & (NG - 1)
-    coarse_cos, coarse_sin = unit_circle(coarse_rows * frequency)
-    fine_cos, fine_sin = unit_circle(fine_rows * frequency)
+    middle_rows = info[0] + FINE * middle + lax.broadcasted_iota(jnp.int32, (FINE, 1), 0)
+    cos_mid, sin_mid = unit_circle((middle_rows & (NG - 1)) * frequency)
+    steps = -(-(middle + 1) // 8) * 8
+    cos_step, sin_step = unit_circle(FINE * lax.broadcasted_iota(jnp.int32, (steps, 1), 0) * frequency)
     spot = slice(far * width, (far + 1) * width)
-    for block in range(rows // FINE):
-        c = coarse_cos[block : block + 1]
-        s = coarse_sin[block : block + 1]
-        place_rows = slice(block * FINE, (block + 1) * FINE)
-        cos_ref[near, place_rows, spot] = (c * fine_cos - s * fine_sin).astype(bf16)
-        sin_ref[near, place_rows, spot] = (s * fine_cos + c * fine_sin).astype(bf16)
+
+    def write(block, cosine, sine):
+        if 0 <= block < blocks:
+            cos_ref[near, block * FINE : (block + 1) * FINE, spot] = cosine.astype(bf16)
+            sin_ref[near, block * FINE : (block + 1) * FINE, spot] = sine.astype(bf16)
+
+    write(middle, cos_mid, sin_mid)
+    for away in range(1, middle + 1):
+        c = cos_step[away : away + 1]
+        s = sin_step[away : away + 1]
+        cc, ss, sc, cs = cos_mid * c, sin_mid * s, sin_mid * c, cos_mid * s
+        write(middle + away, cc - ss, sc + cs)
+        write(middle - away, cc + ss, sc - cs)
 
 
 LIMIT = 8 << 20
+OPENING_LIMIT = 12 << 20
 
 
 def turned(values, cosine, sine, scale):
@@ -338,7 +347,7 @@
             in_specs=[pl.BlockSpec((2, 1, 2, depth, rows), lambda t, info, place: (0, 1 - place[0], 0, 0, 0))],
             out_specs=[WHOLE] * 4,
         ),
-        compiler_params=pltpu.CompilerParams(vmem_limit_bytes=LIMIT),
+        compiler_params=pltpu.CompilerParams(vmem_limit_bytes=OPENING_LIMIT),
         name="opening",
     )(info, place, data)
 
@@ -503,10 +512,13 @@
         copy.wait()
 
 
+OUT_SLOTS = 2
+
+
 def written(lay, kernel, place, operands, earlier, cores, begun):
     _, rows, cells = operands[2].shape
     depth = operands[0].shape[-2]
-    step = tile_of(rows)
+    step = rows // OUT_SLOTS if rows % (OUT_SLOTS * 128) == 0 else rows
     specs = [SCALARS] + [WHOLE] * len(operands)
     if earlier is not None:
         operands = [*operands, earlier]

time: 125 us -> 123 us (0.984)
  Pallas kernels: 50.5 us -> 49 us
  transfers between devices with their start and end apart: 20 -> 20, of which waited for: 8 -> 8; matrix products, arithmetic and copies ran while one was open for 0% -> 0% of each run, Pallas kernels for 28% -> 27%
where the time goes in v3:
time: 123 us; the launch traced here: 122 us
  Pallas kernels  49 us (40%)
  waiting for transfers between devices  48.1 us (39%)
  starting transfers between devices  20.8 us (17%)
  local copies, waits for them, and re-layouts  2.21 us (2%)
  other arithmetic  1.44 us (1%)
    ppermute x20, waiting for transfers between devices, send(): return lax.ppermute(value, AXES, self.along(stage, shift))  48.1 us
    ppermute x20, starting transfers between devices, send(): return lax.ppermute(value, AXES, self.along(stage, shift))  20.8 us
    pallas_call x3, Pallas kernels, written(): pl.pallas_call(kernel, out_shape=[jax.ShapeDtypeStruct((2, lay.high, 2, d...  18 us
    pallas_call x5, Pallas kernels, piece(): pl.pallas_call(kernel, out_shape=[jax.ShapeDtypeStruct((lay.far, 2, depth...  16.9 us
    pallas_call x1, Pallas kernels, opening(): pl.pallas_call(functools.partial(opening_kernel, lay, scale), out_shape=[...  8.04 us
    pallas_call x1, Pallas kernels, begin(): pl.pallas_call(functools.partial(begin_kernel, lay, tile_of(rows)), out_s...  5.16 us
  transfers between devices with their start and end apart: 20, of which 8 were waited for; matrix products, arithmetic and copies ran while one was open for 0% of the time, Pallas kernels for 27%

profile of v3, /device:TPU:0, one launch (start us, length us, event | category | flops | bytes accessed | tf_op | source)
XLA Modules:
  0.0 121.9 jit_solution(631138219380213599)
XLA Ops:
  0.0 0.7 pad_add_fusion.1.info
  0.7 0.1 pad_add_fusion.place
  0.8 2.2 %copy-done = bf16[1,2,512,2048]{3,2,1,0:T(8,128)(2,1)S(1)} copy-done((bf16[1,2,512,2048]{3,2,1,0:T(8,128)(2,1)S(1)}, bf16[1,2,512,2048]{3,2,1,0:T(8,128)(2,1)}, u32[]{:S(2)}) %copy-start) | copy-done | bytes 4194328
  3.0 8.0 %opening.1 = (bf16[4,2,128,256]{3,2,1,0:T(8,128)(2,1)S(1)}, bf16[4,2,128,256]{3,2,1,0:T(8,128)(2,1)S(1)}, bf16[2,2048,1024]{2,1,0:T(8,128)(2,1)S(1)}, bf16[2,2048,1024]{2,1,0:T(8,128)(2,1)S(1)}) custom-call(s32[6]{0:T(128)S(1)} %pad_add_fusion.1.info, s32[4]{0:T(128)S(1)} %pad_add_fusion.place, bf16[2,2,2,128,2048]{4,3,2,1,0:T(8,128)(2,1)S(1)} %bitcast.11), custom_call_target="tpu_custom_call" | custom-call | tf_op jit(solution)/shard_map/opening/pallas_call | solution.py:341
  11.0 0.6 collective-permute-start.4
  11.6 2.9 %piece.9 = bf16[4,2,128,256]{3,2,1,0:T(8,128)(2,1)S(1)} custom-call(s32[4]{0:T(128)S(1)} %pad_add_fusion.place, bf16[2,2,2,128,2048]{4,3,2,1,0:T(8,128)(2,1)S(1)} %bitcast.12, bf16[2,2048,1024]{2,1,0:T(8,128)(2,1)S(1)} %get-tuple-element.19.cos_ref, bf16[2,2048,1024]{2,1,0:T(8,128)(2,1)S(1)} %get-tuple-element.20.sin_ref), custom_call_target="tpu_custom_call" | custom-call | tf_op jit(solution)/shard_map/piece/pallas_call | solution.py:388
  14.5 0.1 collective-permute-start.3
  14.6 2.9 %piece.7 = bf16[4,2,128,256]{3,2,1,0:T(8,128)(2,1)S(1)} custom-call(s32[4]{0:T(128)S(1)} %pad_add_fusion.place, bf16[2,2,2,128,2048]{4,3,2,1,0:T(8,128)(2,1)S(1)} %bitcast.13, bf16[2,2048,1024]{2,1,0:T(8,128)(2,1)S(1)} %get-tuple-element.19.cos_ref, bf16[2,2048,1024]{2,1,0:T(8,128)(2,1)S(1)} %get-tuple-element.20.sin_ref), custom_call_target="tpu_custom_call" | custom-call | tf_op jit(solution)/shard_map/piece/pallas_call | solution.py:388
  17.5 0.5 collective-permute-start.1
  18.1 0.1 add_convert_fusion.1
  18.2 2.6 %collective-permute-start.5 = (bf16[4,2,128,256]{3,2,1,0:T(8,128)(2,1)S(1)}, bf16[4,2,128,256]{3,2,1,0:T(8,128)(2,1)S(1)}, u32[]{:S(2)}, u32[]{:S(2)}) collective-permute-start(bf16[4,2,128,256]{3,2,1,0:T(8,128)(2,1)S(1)} %add_convert_fusion.1), channel_id=1, source_target_pairs={{0,2},{1,5},{2,0},{3,7},{4,6},{5,1},{6,4},{7,3},{8,10},{9,13},{10,... | collective-permute-start | bytes 1572872 | tf_op jit(solution)/shard_map/ppermute | solution.py:81
  20.8 5.3 %piece.5 = (bf16[4,2,128,256]{3,2,1,0:T(8,128)(2,1)S(1)}, bf16[4,2,128,256]{3,2,1,0:T(8,128)(2,1)S(1)}) custom-call(s32[4]{0:T(128)S(1)} %pad_add_fusion.place, bf16[2,2,2,128,2048]{4,3,2,1,0:T(8,128)(2,1)S(1)} %bitcast.14, bf16[2,2048,1024]{2,1,0:T(8,128)(2,1)S(1)} %get-tuple-element.19.cos_ref, bf16[2,2048,1024]{2,1,0:T(8,128)(2,1)S(1)} %get-tuple-element.20.sin_ref), custom_call_target="tpu_custom_call" | custom-call | tf_op jit(solution)/shard_map/piece/pallas_call | solution.py:388
  26.1 0.2 collective-permute-start
  26.3 2.9 %piece.8 = bf16[4,2,128,256]{3,2,1,0:T(8,128)(2,1)S(1)} custom-call(s32[4]{0:T(128)S(1)} %pad_add_fusion.place, bf16[2,2,2,128,2048]{4,3,2,1,0:T(8,128)(2,1)S(1)} %bitcast.15, bf16[2,2048,1024]{2,1,0:T(8,128)(2,1)S(1)} %get-tuple-element.19.cos_ref, bf16[2,2048,1024]{2,1,0:T(8,128)(2,1)S(1)} %get-tuple-element.20.sin_ref), custom_call_target="tpu_custom_call" | custom-call | tf_op jit(solution)/shard_map/piece/pallas_call | solution.py:388
  29.3 2.9 %piece.6 = bf16[4,2,128,256]{3,2,1,0:T(8,128)(2,1)S(1)} custom-call(s32[4]{0:T(128)S(1)} %pad_add_fusion.place, bf16[2,2,2,128,2048]{4,3,2,1,0:T(8,128)(2,1)S(1)} %bitcast.16, bf16[2,2048,1024]{2,1,0:T(8,128)(2,1)S(1)} %get-tuple-element.19.cos_ref, bf16[2,2048,1024]{2,1,0:T(8,128)(2,1)S(1)} %get-tuple-element.20.sin_ref), custom_call_target="tpu_custom_call" | custom-call | tf_op jit(solution)/shard_map/piece/pallas_call | solution.py:388
  32.2 0.0 copy-start.3
  32.2 0.0 copy-start.4
  32.2 0.0 copy-start.2
  32.2 0.1 add_convert_fusion.2
  32.4 1.6 %collective-permute-start.2 = (bf16[4,2,128,256]{3,2,1,0:T(8,128)(2,1)S(1)}, bf16[4,2,128,256]{3,2,1,0:T(8,128)(2,1)S(1)}, u32[]{:S(2)}, u32[]{:S(2)}) collective-permute-start(bf16[4,2,128,256]{3,2,1,0:T(8,128)(2,1)S(1)} %add_convert_fusion.2), channel_id=1, source_target_pairs={{0,2},{1,5},{2,0},{3,7},{4,6},{5,1},{6,4},{7,3},{8,10},{9,13},{10,... | collective-permute-start | bytes 1572872 | tf_op jit(solution)/shard_map/ppermute | solution.py:81
  34.0 0.2 add_convert_fusion
  34.2 0.6 collective-permute-start.6
  34.8 11.6 %collective-permute-done.2.refs_1_ = bf16[4,2,128,256]{3,2,1,0:T(8,128)(2,1)S(1)} collective-permute-done((bf16[4,2,128,256]{3,2,1,0:T(8,128)(2,1)S(1)}, bf16[4,2,128,256]{3,2,1,0:T(8,128)(2,1)S(1)}, u32[]{:S(2)}, u32[]{:S(2)}) %collective-permute-start.2) | collective-permute-done | bytes 524320 | tf_op jit(solution)/shard_map/ppermute | solution.py:81
  46.4 0.2 collective-permute-done.6.refs_2_
  46.6 0.8 blocks.1
  47.4 1.6 %collective-permute-start.7 = (bf16[2,128,256]{2,1,0:T(8,128)(2,1)S(1)}, bf16[2,128,256]{2,1,0:T(8,128)(2,1)S(1)}, u32[]{:S(2)}, u32[]{:S(2)}) collective-permute-start(bf16[2,128,256]{2,1,0:T(8,128)(2,1)S(1)} %get-tuple-element.26), channel_id=1, source_target_pairs={{0,8},{1,9},{2,10},{3,11},{4,12},{5,13},{6,14},{7,15},{8,16},{9,17... | collective-permute-start | bytes 393224 | tf_op jit(solution)/shard_map/ppermute | solution.py:81
  49.0 2.6 %collective-permute-start.8 = (bf16[2,128,256]{2,1,0:T(8,128)(2,1)S(1)}, bf16[2,128,256]{2,1,0:T(8,128)(2,1)S(1)}, u32[]{:S(2)}, u32[]{:S(2)}) collective-permute-start(bf16[2,128,256]{2,1,0:T(8,128)(2,1)S(1)} %get-tuple-element.27), channel_id=1, source_target_pairs={{0,16},{1,17},{2,18},{3,19},{4,20},{5,21},{6,22},{7,23},{8,24},{9,... | collective-permute-start | bytes 393224 | tf_op jit(solution)/shard_map/ppermute | solution.py:81
  51.6 1.3 %collective-permute-start.9 = (bf16[2,128,256]{2,1,0:T(8,128)(2,1)S(1)}, bf16[2,128,256]{2,1,0:T(8,128)(2,1)S(1)}, u32[]{:S(2)}, u32[]{:S(2)}) collective-permute-start(bf16[2,128,256]{2,1,0:T(8,128)(2,1)S(1)} %get-tuple-element.28), channel_id=1, source_target_pairs={{0,24},{1,25},{2,26},{3,27},{4,28},{5,29},{6,30},{7,31},{8,0},{9,1... | collective-permute-start | bytes 393224 | tf_op jit(solution)/shard_map/ppermute | solution.py:81
  53.0 2.7 %collective-permute-done.7 = bf16[2,128,256]{2,1,0:T(8,128)(2,1)S(1)} collective-permute-done((bf16[2,128,256]{2,1,0:T(8,128)(2,1)S(1)}, bf16[2,128,256]{2,1,0:T(8,128)(2,1)S(1)}, u32[]{:S(2)}, u32[]{:S(2)}) %collective-permute-start.7) | collective-permute-done | bytes 131104 | tf_op jit(solution)/shard_map/ppermute | solution.py:81
  55.7 5.1 %collective-permute-done.8 = bf16[2,128,256]{2,1,0:T(8,128)(2,1)S(1)} collective-permute-done((bf16[2,128,256]{2,1,0:T(8,128)(2,1)S(1)}, bf16[2,128,256]{2,1,0:T(8,128)(2,1)S(1)}, u32[]{:S(2)}, u32[]{:S(2)}) %collective-permute-start.8) | collective-permute-done | bytes 131104 | tf_op jit(solution)/shard_map/ppermute | solution.py:81
  60.9 0.1 multiply_convert_fusion
  61.0 3.4 %collective-permute-start.10 = (bf16[2,128,256]{2,1,0:T(8,128)(2,1)S(1)}, bf16[2,128,256]{2,1,0:T(8,128)(2,1)S(1)}, u32[]{:S(2)}, u32[]{:S(2)}) collective-permute-start(bf16[2,128,256]{2,1,0:T(8,128)(2,1)S(1)} %multiply_convert_fusion), channel_id=1, source_target_pairs={{0,8},{1,9},{2,10},{3,11},{4,12},{5,13},{6,14},{7,15},{8,16},{9,17... | collective-permute-start | bytes 393224 | tf_op jit(solution)/shard_map/ppermute | solution.py:81
  64.3 1.6 %collective-permute-start.11 = (bf16[2,128,256]{2,1,0:T(8,128)(2,1)S(1)}, bf16[2,128,256]{2,1,0:T(8,128)(2,1)S(1)}, u32[]{:S(2)}, u32[]{:S(2)}) collective-permute-start(bf16[2,128,256]{2,1,0:T(8,128)(2,1)S(1)} %multiply_convert_fusion), channel_id=1, source_target_pairs={{0,16},{1,17},{2,18},{3,19},{4,20},{5,21},{6,22},{7,23},{8,24},{9,... | collective-permute-start | bytes 393224 | tf_op jit(solution)/shard_map/ppermute | solution.py:81
  65.9 0.8 collective-permute-start.12
  66.8 3.1 %collective-permute-done.10 = bf16[2,128,256]{2,1,0:T(8,128)(2,1)S(1)} collective-permute-done((bf16[2,128,256]{2,1,0:T(8,128)(2,1)S(1)}, bf16[2,128,256]{2,1,0:T(8,128)(2,1)S(1)}, u32[]{:S(2)}, u32[]{:S(2)}) %collective-permute-start.10) | collective-permute-done | bytes 131104 | tf_op jit(solution)/shard_map/ppermute | solution.py:81
  69.8 4.5 %collective-permute-done.11 = bf16[2,128,256]{2,1,0:T(8,128)(2,1)S(1)} collective-permute-done((bf16[2,128,256]{2,1,0:T(8,128)(2,1)S(1)}, bf16[2,128,256]{2,1,0:T(8,128)(2,1)S(1)}, u32[]{:S(2)}, u32[]{:S(2)}) %collective-permute-start.11) | collective-permute-done | bytes 131104 | tf_op jit(solution)/shard_map/ppermute | solution.py:81
  74.4 0.1 pad_maximum_fusion.own
  74.4 1.3 %collective-permute-start.13 = (bf16[4,2,128,256]{3,2,1,0:T(8,128)(2,1)S(1)}, bf16[4,2,128,256]{3,2,1,0:T(8,128)(2,1)S(1)}, u32[]{:S(2)}, u32[]{:S(2)}) collective-permute-start(bf16[4,2,128,256]{3,2,1,0:T(8,128)(2,1)S(1)} %pad_maximum_fusion.own), channel_id=1, source_target_pairs={{0,4},{1,3},{2,6},{3,1},{4,0},{5,7},{6,2},{7,5},{8,12},{9,11},{10,... | collective-permute-start | bytes 1572872 | tf_op jit(solution)/shard_map/ppermute | solution.py:81
  75.7 0.7 collective-permute-start.16
  76.5 12.8 %collective-permute-done.13.own = bf16[4,2,128,256]{3,2,1,0:T(8,128)(2,1)S(1)} collective-permute-done((bf16[4,2,128,256]{3,2,1,0:T(8,128)(2,1)S(1)}, bf16[4,2,128,256]{3,2,1,0:T(8,128)(2,1)S(1)}, u32[]{:S(2)}, u32[]{:S(2)}) %collective-permute-start.13) | collective-permute-done | bytes 524320 | tf_op jit(solution)/shard_map/ppermute | solution.py:81
  89.3 0.7 collective-permute-start.14
  90.0 0.5 collective-permute-start.19
  90.5 0.0 collective-permute-start.17
  90.5 8.0 %collective-permute-done.14.own = bf16[4,2,128,256]{3,2,1,0:T(8,128)(2,1)S(1)} collective-permute-done((bf16[4,2,128,256]{3,2,1,0:T(8,128)(2,1)S(1)}, bf16[4,2,128,256]{3,2,1,0:T(8,128)(2,1)S(1)}, u32[]{:S(2)}, u32[]{:S(2)}) %collective-permute-start.14) | collective-permute-done | bytes 524320 | tf_op jit(solution)/shard_map/ppermute | solution.py:81
  98.5 5.2 %begin.1.total = f32[2,2,128,2048]{3,2,1,0:T(8,128)S(1)} custom-call(s32[4]{0:T(128)S(1)} %pad_add_fusion.place, bf16[4,2,128,256]{3,2,1,0:T(8,128)(2,1)S(1)} %pad_maximum_fusion.own, bf16[4,2,128,256]{3,2,1,0:T(8,128)(2,1)S(1)} %collective-permute-done.18.other, bf16[2,2048,1024]{2,1,0:T(8,128)(2,1)S(1)} %get-tuple-element.19.cos_ref, ...), custom_call_target="tpu_custom_call" | custom-call | tf_op jit(solution)/shard_map/begin/pallas_call | solution.py:460
  103.7 5.7 %shard_map.55 = (bf16[2,2,2,128,2048]{4,3,2,1,0:T(8,128)(2,1)}, f32[2,128,2048]{2,1,0:T(8,128)S(1)}) custom-call(s32[4]{0:T(128)S(1)} %pad_add_fusion.place, bf16[4,2,128,256]{3,2,1,0:T(8,128)(2,1)S(1)} %collective-permute-done.13.own, bf16[4,2,128,256]{3,2,1,0:T(8,128)(2,1)S(1)} %collective-permute-done.19.other, ...), custom_call_target="tpu_custom_call" | custom-call | tf_op jit(solution)/shard_map/pallas_call | solution.py:527
  109.4 5.7 %shard_map.56 = (bf16[2,2,2,128,2048]{4,3,2,1,0:T(8,128)(2,1)}, f32[2,128,2048]{2,1,0:T(8,128)S(1)}) custom-call(s32[4]{0:T(128)S(1)} %pad_add_fusion.place, bf16[4,2,128,256]{3,2,1,0:T(8,128)(2,1)S(1)} %collective-permute-done.16.own, bf16[4,2,128,256]{3,2,1,0:T(8,128)(2,1)S(1)} %collective-permute-done.17.other, ...), custom_call_target="tpu_custom_call", output_to_operand_aliasing={{0}: (6, {})} | custom-call | tf_op jit(solution)/shard_map/pallas_call | solution.py:527
  115.1 6.7 %shard_map.57 = bf16[2,2,2,128,2048]{4,3,2,1,0:T(8,128)(2,1)} custom-call(s32[4]{0:T(128)S(1)} %pad_add_fusion.place, bf16[4,2,128,256]{3,2,1,0:T(8,128)(2,1)S(1)} %collective-permute-done.14.own, bf16[4,2,128,256]{3,2,1,0:T(8,128)(2,1)S(1)} %collective-permute-done.15.other, ...), custom_call_target="tpu_custom_call", output_to_operand_aliasing={{}: (7, {})} | custom-call | tf_op jit(solution)/shard_map/pallas_call | solution.py:527
  (21 shorter events, 0.1 us)
Async XLA Ops:
  0.8 2.2 %copy-start = (bf16[1,2,512,2048]{3,2,1,0:T(8,128)(2,1)S(1)}, bf16[1,2,512,2048]{3,2,1,0:T(8,128)(2,1)}, u32[]{:S(2)}) copy-start(bf16[1,2,512,2048]{3,2,1,0:T(8,128)(2,1)} %param.5) | copy-start | bytes 12582916
  11.0 7.0 %collective-permute-start.4 = (bf16[4,2,128,256]{3,2,1,0:T(8,128)(2,1)S(1)}, bf16[4,2,128,256]{3,2,1,0:T(8,128)(2,1)S(1)}, u32[]{:S(2)}, u32[]{:S(2)}) collective-permute-start(bf16[4,2,128,256]{3,2,1,0:T(8,128)(2,1)S(1)} %get-tuple-element.24), channel_id=1, source_target_pairs={{0,1},{1,0},{2,3},{3,2},{4,5},{5,4},{6,7},{7,6},{8,9},{9,8},{10,11... | collective-permute-start | bytes 1572872 | tf_op jit(solution)/shard_map/ppermute | solution.py:81
  14.5 19.5 %collective-permute-start.3 = (bf16[4,2,128,256]{3,2,1,0:T(8,128)(2,1)S(1)}, bf16[4,2,128,256]{3,2,1,0:T(8,128)(2,1)S(1)}, u32[]{:S(2)}, u32[]{:S(2)}) collective-permute-start(bf16[4,2,128,256]{3,2,1,0:T(8,128)(2,1)S(1)} %piece.9), channel_id=1, source_target_pairs={{0,1},{1,0},{2,3},{3,2},{4,5},{5,4},{6,7},{7,6},{8,9},{9,8},{10,11... | collective-permute-start | bytes 1572872 | tf_op jit(solution)/shard_map/ppermute | solution.py:81
  14.6 6.2 %copy-start.1 = (bf16[1,2,512,2048]{3,2,1,0:T(8,128)(2,1)S(1)}, bf16[1,2,512,2048]{3,2,1,0:T(8,128)(2,1)}, u32[]{:S(2)}) copy-start(bf16[1,2,512,2048]{3,2,1,0:T(8,128)(2,1)} %param.5) | copy-start | bytes 12582916
  17.5 14.7 %collective-permute-start.1 = (bf16[4,2,128,256]{3,2,1,0:T(8,128)(2,1)S(1)}, bf16[4,2,128,256]{3,2,1,0:T(8,128)(2,1)S(1)}, u32[]{:S(2)}, u32[]{:S(2)}) collective-permute-start(bf16[4,2,128,256]{3,2,1,0:T(8,128)(2,1)S(1)} %piece.7), channel_id=1, source_target_pairs={{0,1},{1,0},{2,3},{3,2},{4,5},{5,4},{6,7},{7,6},{8,9},{9,8},{10,11... | collective-permute-start | bytes 1572872 | tf_op jit(solution)/shard_map/ppermute | solution.py:81
  18.2 15.8 %collective-permute-start.5 = (bf16[4,2,128,256]{3,2,1,0:T(8,128)(2,1)S(1)}, bf16[4,2,128,256]{3,2,1,0:T(8,128)(2,1)S(1)}, u32[]{:S(2)}, u32[]{:S(2)}) collective-permute-start(bf16[4,2,128,256]{3,2,1,0:T(8,128)(2,1)S(1)} %add_convert_fusion.1), channel_id=1, source_target_pairs={{0,2},{1,5},{2,0},{3,7},{4,6},{5,1},{6,4},{7,3},{8,10},{9,13},{10,... | collective-permute-start | bytes 1572872 | tf_op jit(solution)/shard_map/ppermute | solution.py:81
  26.1 8.7 %collective-permute-start = (bf16[4,2,128,256]{3,2,1,0:T(8,128)(2,1)S(1)}, bf16[4,2,128,256]{3,2,1,0:T(8,128)(2,1)S(1)}, u32[]{:S(2)}, u32[]{:S(2)}) collective-permute-start(bf16[4,2,128,256]{3,2,1,0:T(8,128)(2,1)S(1)} %get-tuple-element.22), channel_id=1, source_target_pairs={{0,1},{1,0},{2,3},{3,2},{4,5},{5,4},{6,7},{7,6},{8,9},{9,8},{10,11... | collective-permute-start | bytes 1572872 | tf_op jit(solution)/shard_map/ppermute | solution.py:81
  32.2 20.8 %copy-start.3 = (f32[128,256]{1,0:T(8,128)S(1)}, f32[128,256]{1,0:T(8,128)}, u32[]{:S(2)}) copy-start(f32[128,256]{1,0:T(8,128)} %param.8) | copy-start | bytes 393220
  32.2 20.8 %copy-start.4 = (s32[128,256]{1,0:T(8,128)S(1)}, s32[128,256]{1,0:T(8,128)}, u32[]{:S(2)}) copy-start(s32[128,256]{1,0:T(8,128)} %param.9) | copy-start | bytes 393220
  32.2 28.7 %copy-start.2 = (f32[2,128,256]{2,1,0:T(8,128)S(1)}, f32[2,128,256]{2,1,0:T(8,128)}, u32[]{:S(2)}) copy-start(f32[2,128,256]{2,1,0:T(8,128)} %param.7) | copy-start | bytes 786436
  32.4 14.0 %collective-permute-start.2 = (bf16[4,2,128,256]{3,2,1,0:T(8,128)(2,1)S(1)}, bf16[4,2,128,256]{3,2,1,0:T(8,128)(2,1)S(1)}, u32[]{:S(2)}, u32[]{:S(2)}) collective-permute-start(bf16[4,2,128,256]{3,2,1,0:T(8,128)(2,1)S(1)} %add_convert_fusion.2), channel_id=1, source_target_pairs={{0,2},{1,5},{2,0},{3,7},{4,6},{5,1},{6,4},{7,3},{8,10},{9,13},{10,... | collective-permute-start | bytes 1572872 | tf_op jit(solution)/shard_map/ppermute | solution.py:81
  34.2 12.4 %collective-permute-start.6 = (bf16[4,2,128,256]{3,2,1,0:T(8,128)(2,1)S(1)}, bf16[4,2,128,256]{3,2,1,0:T(8,128)(2,1)S(1)}, u32[]{:S(2)}, u32[]{:S(2)}) collective-permute-start(bf16[4,2,128,256]{3,2,1,0:T(8,128)(2,1)S(1)} %add_convert_fusion), channel_id=1, source_target_pairs={{0,4},{1,3},{2,6},{3,1},{4,0},{5,7},{6,2},{7,5},{8,12},{9,11},{10,... | collective-permute-start | bytes 1572872 | tf_op jit(solution)/shard_map/ppermute | solution.py:81
  47.4 8.3 %collective-permute-start.7 = (bf16[2,128,256]{2,1,0:T(8,128)(2,1)S(1)}, bf16[2,128,256]{2,1,0:T(8,128)(2,1)S(1)}, u32[]{:S(2)}, u32[]{:S(2)}) collective-permute-start(bf16[2,128,256]{2,1,0:T(8,128)(2,1)S(1)} %get-tuple-element.26), channel_id=1, source_target_pairs={{0,8},{1,9},{2,10},{3,11},{4,12},{5,13},{6,14},{7,15},{8,16},{9,17... | collective-permute-start | bytes 393224 | tf_op jit(solution)/shard_map/ppermute | solution.py:81
  49.0 11.8 %collective-permute-start.8 = (bf16[2,128,256]{2,1,0:T(8,128)(2,1)S(1)}, bf16[2,128,256]{2,1,0:T(8,128)(2,1)S(1)}, u32[]{:S(2)}, u32[]{:S(2)}) collective-permute-start(bf16[2,128,256]{2,1,0:T(8,128)(2,1)S(1)} %get-tuple-element.27), channel_id=1, source_target_pairs={{0,16},{1,17},{2,18},{3,19},{4,20},{5,21},{6,22},{7,23},{8,24},{9,... | collective-permute-start | bytes 393224 | tf_op jit(solution)/shard_map/ppermute | solution.py:81
  51.6 9.2 %collective-permute-start.9 = (bf16[2,128,256]{2,1,0:T(8,128)(2,1)S(1)}, bf16[2,128,256]{2,1,0:T(8,128)(2,1)S(1)}, u32[]{:S(2)}, u32[]{:S(2)}) collective-permute-start(bf16[2,128,256]{2,1,0:T(8,128)(2,1)S(1)} %get-tuple-element.28), channel_id=1, source_target_pairs={{0,24},{1,25},{2,26},{3,27},{4,28},{5,29},{6,30},{7,31},{8,0},{9,1... | collective-permute-start | bytes 393224 | tf_op jit(solution)/shard_map/ppermute | solution.py:81
  61.0 8.9 %collective-permute-start.10 = (bf16[2,128,256]{2,1,0:T(8,128)(2,1)S(1)}, bf16[2,128,256]{2,1,0:T(8,128)(2,1)S(1)}, u32[]{:S(2)}, u32[]{:S(2)}) collective-permute-start(bf16[2,128,256]{2,1,0:T(8,128)(2,1)S(1)} %multiply_convert_fusion), channel_id=1, source_target_pairs={{0,8},{1,9},{2,10},{3,11},{4,12},{5,13},{6,14},{7,15},{8,16},{9,17... | collective-permute-start | bytes 393224 | tf_op jit(solution)/shard_map/ppermute | solution.py:81
  64.3 10.0 %collective-permute-start.11 = (bf16[2,128,256]{2,1,0:T(8,128)(2,1)S(1)}, bf16[2,128,256]{2,1,0:T(8,128)(2,1)S(1)}, u32[]{:S(2)}, u32[]{:S(2)}) collective-permute-start(bf16[2,128,256]{2,1,0:T(8,128)(2,1)S(1)} %multiply_convert_fusion), channel_id=1, source_target_pairs={{0,16},{1,17},{2,18},{3,19},{4,20},{5,21},{6,22},{7,23},{8,24},{9,... | collective-permute-start | bytes 393224 | tf_op jit(solution)/shard_map/ppermute | solution.py:81
  65.9 8.4 %collective-permute-start.12 = (bf16[2,128,256]{2,1,0:T(8,128)(2,1)S(1)}, bf16[2,128,256]{2,1,0:T(8,128)(2,1)S(1)}, u32[]{:S(2)}, u32[]{:S(2)}) collective-permute-start(bf16[2,128,256]{2,1,0:T(8,128)(2,1)S(1)} %multiply_convert_fusion), channel_id=1, source_target_pairs={{0,24},{1,25},{2,26},{3,27},{4,28},{5,29},{6,30},{7,31},{8,0},{9,1... | collective-permute-start | bytes 393224 | tf_op jit(solution)/shard_map/ppermute | solution.py:81
  74.4 14.9 %collective-permute-start.13 = (bf16[4,2,128,256]{3,2,1,0:T(8,128)(2,1)S(1)}, bf16[4,2,128,256]{3,2,1,0:T(8,128)(2,1)S(1)}, u32[]{:S(2)}, u32[]{:S(2)}) collective-permute-start(bf16[4,2,128,256]{3,2,1,0:T(8,128)(2,1)S(1)} %pad_maximum_fusion.own), channel_id=1, source_target_pairs={{0,4},{1,3},{2,6},{3,1},{4,0},{5,7},{6,2},{7,5},{8,12},{9,11},{10,... | collective-permute-start | bytes 1572872 | tf_op jit(solution)/shard_map/ppermute | solution.py:81
  75.7 14.8 %collective-permute-start.16 = (bf16[4,2,128,256]{3,2,1,0:T(8,128)(2,1)S(1)}, bf16[4,2,128,256]{3,2,1,0:T(8,128)(2,1)S(1)}, u32[]{:S(2)}, u32[]{:S(2)}) collective-permute-start(bf16[4,2,128,256]{3,2,1,0:T(8,128)(2,1)S(1)} %pad_maximum_fusion.own), channel_id=1, source_target_pairs={{0,2},{1,5},{2,0},{3,7},{4,6},{5,1},{6,4},{7,3},{8,10},{9,13},{10,... | collective-permute-start | bytes 1572872 | tf_op jit(solution)/shard_map/ppermute | solution.py:81
  89.3 9.2 %collective-permute-start.14 = (bf16[4,2,128,256]{3,2,1,0:T(8,128)(2,1)S(1)}, bf16[4,2,128,256]{3,2,1,0:T(8,128)(2,1)S(1)}, u32[]{:S(2)}, u32[]{:S(2)}) collective-permute-start(bf16[4,2,128,256]{3,2,1,0:T(8,128)(2,1)S(1)} %collective-permute-done.13.own), channel_id=1, source_target_pairs={{0,2},{1,5},{2,0},{3,7},{4,6},{5,1},{6,4},{7,3},{8,10},{9,13},{10,... | collective-permute-start | bytes 1572872 | tf_op jit(solution)/shard_map/ppermute | solution.py:81
  90.0 8.5 %collective-permute-start.18 = (bf16[4,2,128,256]{3,2,1,0:T(8,128)(2,1)S(1)}, bf16[4,2,128,256]{3,2,1,0:T(8,128)(2,1)S(1)}, u32[]{:S(2)}, u32[]{:S(2)}) collective-permute-start(bf16[4,2,128,256]{3,2,1,0:T(8,128)(2,1)S(1)} %pad_maximum_fusion.own), channel_id=1, source_target_pairs={{0,1},{1,0},{2,3},{3,2},{4,5},{5,4},{6,7},{7,6},{8,9},{9,8},{10,11... | collective-permute-start | bytes 1572872 | tf_op jit(solution)/shard_map/ppermute | solution.py:81
  90.0 13.7 %collective-permute-start.19 = (bf16[4,2,128,256]{3,2,1,0:T(8,128)(2,1)S(1)}, bf16[4,2,128,256]{3,2,1,0:T(8,128)(2,1)S(1)}, u32[]{:S(2)}, u32[]{:S(2)}) collective-permute-start(bf16[4,2,128,256]{3,2,1,0:T(8,128)(2,1)S(1)} %collective-permute-done.13.own), channel_id=1, source_target_pairs={{0,1},{1,0},{2,3},{3,2},{4,5},{5,4},{6,7},{7,6},{8,9},{9,8},{10,11... | collective-permute-start | bytes 1572872 | tf_op jit(solution)/shard_map/ppermute | solution.py:81
  90.5 18.9 %collective-permute-start.17 = (bf16[4,2,128,256]{3,2,1,0:T(8,128)(2,1)S(1)}, bf16[4,2,128,256]{3,2,1,0:T(8,128)(2,1)S(1)}, u32[]{:S(2)}, u32[]{:S(2)}) collective-permute-start(bf16[4,2,128,256]{3,2,1,0:T(8,128)(2,1)S(1)} %collective-permute-done.16.own), channel_id=1, source_target_pairs={{0,1},{1,0},{2,3},{3,2},{4,5},{5,4},{6,7},{7,6},{8,9},{9,8},{10,11... | collective-permute-start | bytes 1572872 | tf_op jit(solution)/shard_map/ppermute | solution.py:81
  98.5 16.6 %collective-permute-start.15 = (bf16[4,2,128,256]{3,2,1,0:T(8,128)(2,1)S(1)}, bf16[4,2,128,256]{3,2,1,0:T(8,128)(2,1)S(1)}, u32[]{:S(2)}, u32[]{:S(2)}) collective-permute-start(bf16[4,2,128,256]{3,2,1,0:T(8,128)(2,1)S(1)} %collective-permute-done.14.own), channel_id=1, source_target_pairs={{0,1},{1,0},{2,3},{3,2},{4,5},{5,4},{6,7},{7,6},{8,9},{9,8},{10,11... | collective-permute-start | bytes 1572872 | tf_op jit(solution)/shard_map/ppermute | solution.py:81

commit v4 on v3

--- a/solution.py
+++ b/solution.py
@@ -323,7 +323,7 @@
 def opening_kernel(lay, scale, info, place, data, away, keep, cos_ref, sin_ref):
     width = away.shape[-1]
     cores = (1 - place[1], place[1])
-    values = jnp.concatenate([data[part, 0, core] for part in range(2) for core in cores], axis=0)
+    values = jnp.concatenate([data[part, core] for part in range(2) for core in cores], axis=0)
     fill = functools.partial(table_tile, lay, info, place, cos_ref, sin_ref, width=width)
     fill(0, 0)
     for far in range(lay.far):
@@ -341,13 +341,14 @@
     return pl.pallas_call(
         functools.partial(opening_kernel, lay, scale),
         out_shape=[half] * 2 + [pltpu.VMEM((2, rows, total), bf16)] * 2,
-        grid_spec=pltpu.PrefetchScalarGridSpec(
-            num_scalar_prefetch=2,
-            grid=(1,),
-            in_specs=[pl.BlockSpec((2, 1, 2, depth, rows), lambda t, info, place: (0, 1 - place[0], 0, 0, 0))],
-            out_specs=[WHOLE] * 4,
+        in_specs=[SCALARS] * 2 + [WHOLE],
+        out_specs=[WHOLE] * 4,
+        compiler_params=pltpu.CompilerParams(vmem_limit_bytes=OPENING_LIMIT),
+        cost_estimate=pl.CostEstimate(
+            flops=16 * depth * rows * total + 16 * rows * total,
+            transcendentals=0,
+            bytes_accessed=8 * rows * total,
         ),
-        compiler_params=pltpu.CompilerParams(vmem_limit_bytes=OPENING_LIMIT),
         name="opening",
     )(info, place, data)
 
@@ -570,7 +571,8 @@
     def side(first, other):
         return piece(lay, functools.partial(side_kernel, lay, scale, first, other), 1, place, data, tables, width)[0]
 
-    away, keep, *tables = opening(lay, scale, info, place, data, width)
+    others = lax.dynamic_index_in_dim(data, 1 - high, 1, keepdims=False)
+    away, keep, *tables = opening(lay, scale, info, place, others, width)
     cross = sent("core", away)
     away = side(0, True)
     first_a = sent("first", keep, cross)
@@ -592,7 +594,10 @@
     def paired(value):
         return [value, sent("core", value)]
 
-    corner = gather_stage(lay, residual, "far", lay.far)
+    arrived = [residual]
+    for shift in range(1, lay.far):
+        arrived.append(lay.send(residual, "far", shift))
+    corner = jnp.stack(arrived)
     over_second = sent("second", corner)
     corners = paired(corner)
     total = begin(lay, corners, tables, place)

time: 123 us -> 124 us (level)
  waiting for transfers between devices: 48.1 us -> 52.7 us
  starting transfers between devices: 20.8 us -> 19.5 us
    ppermute x20, waiting for transfers between devices: 48.1 us -> 52.7 us  [send(): return lax.ppermute(value, AXES, self.along(stage, shift))]
    unnamed x10, local copies, waits for them, and re-layouts: 2.21 us -> 0.03 us
    squeeze x0 -> x1, local copies, waits for them, and re-layouts: none -> 1.74 us  [in_pieces(): others = lax.dynamic_index_in_dim(data, 1 - high, 1, keepdims=False)]
    ppermute x20, starting transfers between devices: 20.8 us -> 19.5 us  [send(): return lax.ppermute(value, AXES, self.along(stage, shift))]
  transfers between devices with their start and end apart: 20 -> 20, of which waited for: 8 -> 9; matrix products, arithmetic and copies ran while one was open for 0% -> 0% of each run, Pallas kernels for 27% -> 27%
where the time goes in v4:
time: 124 us; the launch traced here: 123 us
  waiting for transfers between devices  52.7 us (42%)
  Pallas kernels  48.3 us (39%)
  starting transfers between devices  19.5 us (16%)
  local copies, waits for them, and re-layouts  1.77 us (1%)
    ppermute x20, waiting for transfers between devices, send(): return lax.ppermute(value, AXES, self.along(stage, shift))  52.7 us
    ppermute x20, starting transfers between devices, send(): return lax.ppermute(value, AXES, self.along(stage, shift))  19.5 us
    pallas_call x3, Pallas kernels, written(): pl.pallas_call(kernel, out_shape=[jax.ShapeDtypeStruct((2, lay.high, 2, d...  17.8 us
    pallas_call x5, Pallas kernels, piece(): pl.pallas_call(kernel, out_shape=[jax.ShapeDtypeStruct((lay.far, 2, depth...  16.7 us
    pallas_call x1, Pallas kernels, opening(): pl.pallas_call(functools.partial(opening_kernel, lay, scale), out_shape=[...  7.92 us
    pallas_call x1, Pallas kernels, begin(): pl.pallas_call(functools.partial(begin_kernel, lay, tile_of(rows)), out_s...  5.16 us
  transfers between devices with their start and end apart: 20, of which 9 were waited for; matrix products, arithmetic and copies ran while one was open for 0% of the time, Pallas kernels for 27%

profile of v4, /device:TPU:0, one launch (start us, length us, event | category | flops | bytes accessed | tf_op | source)
XLA Modules:
  0.0 123.5 jit_solution(5418350333232353922)
XLA Ops:
  0.0 1.7 %dynamic-slice_bitcast_fusion.data = bf16[2,2,128,2048]{3,2,1,0:T(8,128)(2,1)S(1)} fusion(bf16[2,2,2,128,2048]{4,3,2,1,0:T(8,128)(2,1)} %bitcast.13, s32[]{:T(128)S(6)} %select_n.31), kind=kLoop, calls=%fused_computation | loop fusion | bytes 4194308 | tf_op jit(solution)/shard_map/jit(dynamic_index_in_dim)/squeeze | solution.py:574
  1.8 0.1 pad_add_fusion.1.info
  1.9 0.1 pad_add_fusion.place
  1.9 7.9 %opening.1 = (bf16[4,2,128,256]{3,2,1,0:T(8,128)(2,1)S(1)}, bf16[4,2,128,256]{3,2,1,0:T(8,128)(2,1)S(1)}, bf16[2,2048,1024]{2,1,0:T(8,128)(2,1)S(1)}, bf16[2,2048,1024]{2,1,0:T(8,128)(2,1)S(1)}) custom-call(s32[6]{0:T(128)S(1)} %pad_add_fusion.1.info, s32[4]{0:T(128)S(1)} %pad_add_fusion.place, bf16[2,2,128,2048]{3,2,1,0:T(8,128)(2,1)S(1)} %dynamic-slice_bitcast_fusion.data), custom_call_target="tpu_custom_call" | custom-call | flops 4328521728 | bytes 16777216 | tf_op jit(solution)/shard_map/opening/pallas_call | solution.py:341
  9.9 0.6 collective-permute-start.4
  10.4 2.9 %piece.9 = bf16[4,2,128,256]{3,2,1,0:T(8,128)(2,1)S(1)} custom-call(s32[4]{0:T(128)S(1)} %pad_add_fusion.place, bf16[2,2,2,128,2048]{4,3,2,1,0:T(8,128)(2,1)S(1)} %bitcast.14, bf16[2,2048,1024]{2,1,0:T(8,128)(2,1)S(1)} %get-tuple-element.19.cos_ref, bf16[2,2048,1024]{2,1,0:T(8,128)(2,1)S(1)} %get-tuple-element.20.sin_ref), custom_call_target="tpu_custom_call" | custom-call | tf_op jit(solution)/shard_map/piece/pallas_call | solution.py:389
  13.3 0.1 collective-permute-start.3
  13.4 2.9 %piece.7 = bf16[4,2,128,256]{3,2,1,0:T(8,128)(2,1)S(1)} custom-call(s32[4]{0:T(128)S(1)} %pad_add_fusion.place, bf16[2,2,2,128,2048]{4,3,2,1,0:T(8,128)(2,1)S(1)} %bitcast.15, bf16[2,2048,1024]{2,1,0:T(8,128)(2,1)S(1)} %get-tuple-element.19.cos_ref, bf16[2,2048,1024]{2,1,0:T(8,128)(2,1)S(1)} %get-tuple-element.20.sin_ref), custom_call_target="tpu_custom_call" | custom-call | tf_op jit(solution)/shard_map/piece/pallas_call | solution.py:389
  16.3 0.6 collective-permute-start.1
  16.8 0.0 collective-permute-done.4
  16.8 0.1 add_convert_fusion.1
  17.0 2.6 %collective-permute-start.5 = (bf16[4,2,128,256]{3,2,1,0:T(8,128)(2,1)S(1)}, bf16[4,2,128,256]{3,2,1,0:T(8,128)(2,1)S(1)}, u32[]{:S(2)}, u32[]{:S(2)}) collective-permute-start(bf16[4,2,128,256]{3,2,1,0:T(8,128)(2,1)S(1)} %add_convert_fusion.1), channel_id=1, source_target_pairs={{0,2},{1,5},{2,0},{3,7},{4,6},{5,1},{6,4},{7,3},{8,10},{9,13},{10,... | collective-permute-start | bytes 1572872 | tf_op jit(solution)/shard_map/ppermute | solution.py:81
  19.6 5.2 %piece.5 = (bf16[4,2,128,256]{3,2,1,0:T(8,128)(2,1)S(1)}, bf16[4,2,128,256]{3,2,1,0:T(8,128)(2,1)S(1)}) custom-call(s32[4]{0:T(128)S(1)} %pad_add_fusion.place, bf16[2,2,2,128,2048]{4,3,2,1,0:T(8,128)(2,1)S(1)} %bitcast.16, bf16[2,2048,1024]{2,1,0:T(8,128)(2,1)S(1)} %get-tuple-element.19.cos_ref, bf16[2,2048,1024]{2,1,0:T(8,128)(2,1)S(1)} %get-tuple-element.20.sin_ref), custom_call_target="tpu_custom_call" | custom-call | tf_op jit(solution)/shard_map/piece/pallas_call | solution.py:389
  24.8 0.2 collective-permute-start
  25.0 2.9 %piece.8 = bf16[4,2,128,256]{3,2,1,0:T(8,128)(2,1)S(1)} custom-call(s32[4]{0:T(128)S(1)} %pad_add_fusion.place, bf16[2,2,2,128,2048]{4,3,2,1,0:T(8,128)(2,1)S(1)} %bitcast.17, bf16[2,2048,1024]{2,1,0:T(8,128)(2,1)S(1)} %get-tuple-element.19.cos_ref, bf16[2,2048,1024]{2,1,0:T(8,128)(2,1)S(1)} %get-tuple-element.20.sin_ref), custom_call_target="tpu_custom_call" | custom-call | tf_op jit(solution)/shard_map/piece/pallas_call | solution.py:389
  27.9 2.9 %piece.6 = bf16[4,2,128,256]{3,2,1,0:T(8,128)(2,1)S(1)} custom-call(s32[4]{0:T(128)S(1)} %pad_add_fusion.place, bf16[2,2,2,128,2048]{4,3,2,1,0:T(8,128)(2,1)S(1)} %bitcast.18, bf16[2,2048,1024]{2,1,0:T(8,128)(2,1)S(1)} %get-tuple-element.19.cos_ref, bf16[2,2048,1024]{2,1,0:T(8,128)(2,1)S(1)} %get-tuple-element.20.sin_ref), custom_call_target="tpu_custom_call" | custom-call | tf_op jit(solution)/shard_map/piece/pallas_call | solution.py:389
  30.8 0.0 copy-start.2
  30.8 0.0 copy-start.3
  30.8 0.0 copy-start.1
  30.8 0.1 add_convert_fusion.2
  31.0 1.6 %collective-permute-start.2 = (bf16[4,2,128,256]{3,2,1,0:T(8,128)(2,1)S(1)}, bf16[4,2,128,256]{3,2,1,0:T(8,128)(2,1)S(1)}, u32[]{:S(2)}, u32[]{:S(2)}) collective-permute-start(bf16[4,2,128,256]{3,2,1,0:T(8,128)(2,1)S(1)} %add_convert_fusion.2), channel_id=1, source_target_pairs={{0,2},{1,5},{2,0},{3,7},{4,6},{5,1},{6,4},{7,3},{8,10},{9,13},{10,... | collective-permute-start | bytes 1572872 | tf_op jit(solution)/shard_map/ppermute | solution.py:81
  32.6 0.2 add_convert_fusion
  32.8 0.6 collective-permute-start.6
  33.4 11.6 %collective-permute-done.2.refs_1_ = bf16[4,2,128,256]{3,2,1,0:T(8,128)(2,1)S(1)} collective-permute-done((bf16[4,2,128,256]{3,2,1,0:T(8,128)(2,1)S(1)}, bf16[4,2,128,256]{3,2,1,0:T(8,128)(2,1)S(1)}, u32[]{:S(2)}, u32[]{:S(2)}) %collective-permute-start.2) | collective-permute-done | bytes 524320 | tf_op jit(solution)/shard_map/ppermute | solution.py:81
  45.0 0.2 collective-permute-done.6.refs_2_
  45.2 0.8 blocks.1
  46.0 1.6 %collective-permute-start.7 = (bf16[2,128,256]{2,1,0:T(8,128)(2,1)S(1)}, bf16[2,128,256]{2,1,0:T(8,128)(2,1)S(1)}, u32[]{:S(2)}, u32[]{:S(2)}) collective-permute-start(bf16[2,128,256]{2,1,0:T(8,128)(2,1)S(1)} %get-tuple-element.26), channel_id=1, source_target_pairs={{0,8},{1,9},{2,10},{3,11},{4,12},{5,13},{6,14},{7,15},{8,16},{9,17... | collective-permute-start | bytes 393224 | tf_op jit(solution)/shard_map/ppermute | solution.py:81
  47.6 2.6 %collective-permute-start.8 = (bf16[2,128,256]{2,1,0:T(8,128)(2,1)S(1)}, bf16[2,128,256]{2,1,0:T(8,128)(2,1)S(1)}, u32[]{:S(2)}, u32[]{:S(2)}) collective-permute-start(bf16[2,128,256]{2,1,0:T(8,128)(2,1)S(1)} %get-tuple-element.27), channel_id=1, source_target_pairs={{0,16},{1,17},{2,18},{3,19},{4,20},{5,21},{6,22},{7,23},{8,24},{9,... | collective-permute-start | bytes 393224 | tf_op jit(solution)/shard_map/ppermute | solution.py:81
  50.2 1.3 %collective-permute-start.9 = (bf16[2,128,256]{2,1,0:T(8,128)(2,1)S(1)}, bf16[2,128,256]{2,1,0:T(8,128)(2,1)S(1)}, u32[]{:S(2)}, u32[]{:S(2)}) collective-permute-start(bf16[2,128,256]{2,1,0:T(8,128)(2,1)S(1)} %get-tuple-element.28), channel_id=1, source_target_pairs={{0,24},{1,25},{2,26},{3,27},{4,28},{5,29},{6,30},{7,31},{8,0},{9,1... | collective-permute-start | bytes 393224 | tf_op jit(solution)/shard_map/ppermute | solution.py:81
  51.6 2.7 %collective-permute-done.7 = bf16[2,128,256]{2,1,0:T(8,128)(2,1)S(1)} collective-permute-done((bf16[2,128,256]{2,1,0:T(8,128)(2,1)S(1)}, bf16[2,128,256]{2,1,0:T(8,128)(2,1)S(1)}, u32[]{:S(2)}, u32[]{:S(2)}) %collective-permute-start.7) | collective-permute-done | bytes 131104 | tf_op jit(solution)/shard_map/ppermute | solution.py:81
  54.3 5.1 %collective-permute-done.8 = bf16[2,128,256]{2,1,0:T(8,128)(2,1)S(1)} collective-permute-done((bf16[2,128,256]{2,1,0:T(8,128)(2,1)S(1)}, bf16[2,128,256]{2,1,0:T(8,128)(2,1)S(1)}, u32[]{:S(2)}, u32[]{:S(2)}) %collective-permute-start.8) | collective-permute-done | bytes 131104 | tf_op jit(solution)/shard_map/ppermute | solution.py:81
  59.5 0.1 multiply_convert_fusion
  59.6 4.4 %collective-permute-start.12 = (bf16[2,128,256]{2,1,0:T(8,128)(2,1)S(1)}, bf16[2,128,256]{2,1,0:T(8,128)(2,1)S(1)}, u32[]{:S(2)}, u32[]{:S(2)}) collective-permute-start(bf16[2,128,256]{2,1,0:T(8,128)(2,1)S(1)} %multiply_convert_fusion), channel_id=1, source_target_pairs={{0,24},{1,25},{2,26},{3,27},{4,28},{5,29},{6,30},{7,31},{8,0},{9,1... | collective-permute-start | bytes 393224 | tf_op jit(solution)/shard_map/ppermute | solution.py:81
  64.0 0.6 collective-permute-start.11
  64.6 3.3 %collective-permute-done.12 = bf16[2,128,256]{2,1,0:T(8,128)(2,1)S(1)} collective-permute-done((bf16[2,128,256]{2,1,0:T(8,128)(2,1)S(1)}, bf16[2,128,256]{2,1,0:T(8,128)(2,1)S(1)}, u32[]{:S(2)}, u32[]{:S(2)}) %collective-permute-start.12) | collective-permute-done | bytes 131104 | tf_op jit(solution)/shard_map/ppermute | solution.py:81
  67.9 4.1 %collective-permute-done.10 = bf16[2,128,256]{2,1,0:T(8,128)(2,1)S(1)} collective-permute-done((bf16[2,128,256]{2,1,0:T(8,128)(2,1)S(1)}, bf16[2,128,256]{2,1,0:T(8,128)(2,1)S(1)}, u32[]{:S(2)}, u32[]{:S(2)}) %collective-permute-start.10) | collective-permute-done | bytes 131104 | tf_op jit(solution)/shard_map/ppermute | solution.py:81
  72.0 4.2 %collective-permute-done.11 = bf16[2,128,256]{2,1,0:T(8,128)(2,1)S(1)} collective-permute-done((bf16[2,128,256]{2,1,0:T(8,128)(2,1)S(1)}, bf16[2,128,256]{2,1,0:T(8,128)(2,1)S(1)}, u32[]{:S(2)}, u32[]{:S(2)}) %collective-permute-start.11) | collective-permute-done | bytes 131104 | tf_op jit(solution)/shard_map/ppermute | solution.py:81
  76.2 0.1 pad_maximum_fusion.own
  76.3 1.6 %collective-permute-start.13 = (bf16[4,2,128,256]{3,2,1,0:T(8,128)(2,1)S(1)}, bf16[4,2,128,256]{3,2,1,0:T(8,128)(2,1)S(1)}, u32[]{:S(2)}, u32[]{:S(2)}) collective-permute-start(bf16[4,2,128,256]{3,2,1,0:T(8,128)(2,1)S(1)} %pad_maximum_fusion.own), channel_id=1, source_target_pairs={{0,4},{1,3},{2,6},{3,1},{4,0},{5,7},{6,2},{7,5},{8,12},{9,11},{10,... | collective-permute-start | bytes 1572872 | tf_op jit(solution)/shard_map/ppermute | solution.py:81
  77.9 0.5 collective-permute-start.16
  78.4 12.7 %collective-permute-done.13.own = bf16[4,2,128,256]{3,2,1,0:T(8,128)(2,1)S(1)} collective-permute-done((bf16[4,2,128,256]{3,2,1,0:T(8,128)(2,1)S(1)}, bf16[4,2,128,256]{3,2,1,0:T(8,128)(2,1)S(1)}, u32[]{:S(2)}, u32[]{:S(2)}) %collective-permute-start.13) | collective-permute-done | bytes 524320 | tf_op jit(solution)/shard_map/ppermute | solution.py:81
  91.2 0.5 collective-permute-start.19
  91.7 0.0 collective-permute-start.17
  91.7 8.7 %collective-permute-done.14.own = bf16[4,2,128,256]{3,2,1,0:T(8,128)(2,1)S(1)} collective-permute-done((bf16[4,2,128,256]{3,2,1,0:T(8,128)(2,1)S(1)}, bf16[4,2,128,256]{3,2,1,0:T(8,128)(2,1)S(1)}, u32[]{:S(2)}, u32[]{:S(2)}) %collective-permute-start.14) | collective-permute-done | bytes 524320 | tf_op jit(solution)/shard_map/ppermute | solution.py:81
  100.3 5.2 %begin.1.total = f32[2,2,128,2048]{3,2,1,0:T(8,128)S(1)} custom-call(s32[4]{0:T(128)S(1)} %pad_add_fusion.place, bf16[4,2,128,256]{3,2,1,0:T(8,128)(2,1)S(1)} %pad_maximum_fusion.own, bf16[4,2,128,256]{3,2,1,0:T(8,128)(2,1)S(1)} %collective-permute-done.18.other, bf16[2,2048,1024]{2,1,0:T(8,128)(2,1)S(1)} %get-tuple-element.19.cos_ref, ...), custom_call_target="tpu_custom_call" | custom-call | tf_op jit(solution)/shard_map/begin/pallas_call | solution.py:461
  105.5 5.6 %shard_map.55 = (bf16[2,2,2,128,2048]{4,3,2,1,0:T(8,128)(2,1)}, f32[2,128,2048]{2,1,0:T(8,128)S(1)}) custom-call(s32[4]{0:T(128)S(1)} %pad_add_fusion.place, bf16[4,2,128,256]{3,2,1,0:T(8,128)(2,1)S(1)} %collective-permute-done.13.own, bf16[4,2,128,256]{3,2,1,0:T(8,128)(2,1)S(1)} %collective-permute-done.19.other, ...), custom_call_target="tpu_custom_call" | custom-call | tf_op jit(solution)/shard_map/pallas_call | solution.py:528
  111.1 5.6 %shard_map.56 = (bf16[2,2,2,128,2048]{4,3,2,1,0:T(8,128)(2,1)}, f32[2,128,2048]{2,1,0:T(8,128)S(1)}) custom-call(s32[4]{0:T(128)S(1)} %pad_add_fusion.place, bf16[4,2,128,256]{3,2,1,0:T(8,128)(2,1)S(1)} %collective-permute-done.16.own, bf16[4,2,128,256]{3,2,1,0:T(8,128)(2,1)S(1)} %collective-permute-done.17.other, ...), custom_call_target="tpu_custom_call", output_to_operand_aliasing={{0}: (6, {})} | custom-call | tf_op jit(solution)/shard_map/pallas_call | solution.py:528
  116.8 6.6 %shard_map.57 = bf16[2,2,2,128,2048]{4,3,2,1,0:T(8,128)(2,1)} custom-call(s32[4]{0:T(128)S(1)} %pad_add_fusion.place, bf16[4,2,128,256]{3,2,1,0:T(8,128)(2,1)S(1)} %collective-permute-done.14.own, bf16[4,2,128,256]{3,2,1,0:T(8,128)(2,1)S(1)} %collective-permute-done.15.other, ...), custom_call_target="tpu_custom_call", output_to_operand_aliasing={{}: (7, {})} | custom-call | tf_op jit(solution)/shard_map/pallas_call | solution.py:528
  (22 shorter events, 0.1 us)
Async XLA Ops:
  0.0 1.8 %copy-start.4 = (s32[4]{0:T(128)S(1)}, s32[4]{0:T(128)}, u32[]{:S(2)}) copy-start(s32[4]{0:T(128)} %param.6) | copy-start | bytes 52
  1.9 8.5 %copy-start = (bf16[1,2,512,2048]{3,2,1,0:T(8,128)(2,1)S(1)}, bf16[1,2,512,2048]{3,2,1,0:T(8,128)(2,1)}, u32[]{:S(2)}) copy-start(bf16[1,2,512,2048]{3,2,1,0:T(8,128)(2,1)} %param.5) | copy-start | bytes 12582916
  9.9 7.0 %collective-permute-start.4 = (bf16[4,2,128,256]{3,2,1,0:T(8,128)(2,1)S(1)}, bf16[4,2,128,256]{3,2,1,0:T(8,128)(2,1)S(1)}, u32[]{:S(2)}, u32[]{:S(2)}) collective-permute-start(bf16[4,2,128,256]{3,2,1,0:T(8,128)(2,1)S(1)} %get-tuple-element.24), channel_id=1, source_target_pairs={{0,1},{1,0},{2,3},{3,2},{4,5},{5,4},{6,7},{7,6},{8,9},{9,8},{10,11... | collective-permute-start | bytes 1572872 | tf_op jit(solution)/shard_map/ppermute | solution.py:81
  13.3 19.3 %collective-permute-start.3 = (bf16[4,2,128,256]{3,2,1,0:T(8,128)(2,1)S(1)}, bf16[4,2,128,256]{3,2,1,0:T(8,128)(2,1)S(1)}, u32[]{:S(2)}, u32[]{:S(2)}) collective-permute-start(bf16[4,2,128,256]{3,2,1,0:T(8,128)(2,1)S(1)} %piece.9), channel_id=1, source_target_pairs={{0,1},{1,0},{2,3},{3,2},{4,5},{5,4},{6,7},{7,6},{8,9},{9,8},{10,11... | collective-permute-start | bytes 1572872 | tf_op jit(solution)/shard_map/ppermute | solution.py:81
  16.3 14.5 %collective-permute-start.1 = (bf16[4,2,128,256]{3,2,1,0:T(8,128)(2,1)S(1)}, bf16[4,2,128,256]{3,2,1,0:T(8,128)(2,1)S(1)}, u32[]{:S(2)}, u32[]{:S(2)}) collective-permute-start(bf16[4,2,128,256]{3,2,1,0:T(8,128)(2,1)S(1)} %piece.7), channel_id=1, source_target_pairs={{0,1},{1,0},{2,3},{3,2},{4,5},{5,4},{6,7},{7,6},{8,9},{9,8},{10,11... | collective-permute-start | bytes 1572872 | tf_op jit(solution)/shard_map/ppermute | solution.py:81
  17.0 15.6 %collective-permute-start.5 = (bf16[4,2,128,256]{3,2,1,0:T(8,128)(2,1)S(1)}, bf16[4,2,128,256]{3,2,1,0:T(8,128)(2,1)S(1)}, u32[]{:S(2)}, u32[]{:S(2)}) collective-permute-start(bf16[4,2,128,256]{3,2,1,0:T(8,128)(2,1)S(1)} %add_convert_fusion.1), channel_id=1, source_target_pairs={{0,2},{1,5},{2,0},{3,7},{4,6},{5,1},{6,4},{7,3},{8,10},{9,13},{10,... | collective-permute-start | bytes 1572872 | tf_op jit(solution)/shard_map/ppermute | solution.py:81
  24.8 8.6 %collective-permute-start = (bf16[4,2,128,256]{3,2,1,0:T(8,128)(2,1)S(1)}, bf16[4,2,128,256]{3,2,1,0:T(8,128)(2,1)S(1)}, u32[]{:S(2)}, u32[]{:S(2)}) collective-permute-start(bf16[4,2,128,256]{3,2,1,0:T(8,128)(2,1)S(1)} %get-tuple-element.22), channel_id=1, source_target_pairs={{0,1},{1,0},{2,3},{3,2},{4,5},{5,4},{6,7},{7,6},{8,9},{9,8},{10,11... | collective-permute-start | bytes 1572872 | tf_op jit(solution)/shard_map/ppermute | solution.py:81
  30.8 20.8 %copy-start.2 = (f32[128,256]{1,0:T(8,128)S(1)}, f32[128,256]{1,0:T(8,128)}, u32[]{:S(2)}) copy-start(f32[128,256]{1,0:T(8,128)} %param.8) | copy-start | bytes 393220
  30.8 20.8 %copy-start.3 = (s32[128,256]{1,0:T(8,128)S(1)}, s32[128,256]{1,0:T(8,128)}, u32[]{:S(2)}) copy-start(s32[128,256]{1,0:T(8,128)} %param.9) | copy-start | bytes 393220
  30.8 28.7 %copy-start.1 = (f32[2,128,256]{2,1,0:T(8,128)S(1)}, f32[2,128,256]{2,1,0:T(8,128)}, u32[]{:S(2)}) copy-start(f32[2,128,256]{2,1,0:T(8,128)} %param.7) | copy-start | bytes 786436
  31.0 14.0 %collective-permute-start.2 = (bf16[4,2,128,256]{3,2,1,0:T(8,128)(2,1)S(1)}, bf16[4,2,128,256]{3,2,1,0:T(8,128)(2,1)S(1)}, u32[]{:S(2)}, u32[]{:S(2)}) collective-permute-start(bf16[4,2,128,256]{3,2,1,0:T(8,128)(2,1)S(1)} %add_convert_fusion.2), channel_id=1, source_target_pairs={{0,2},{1,5},{2,0},{3,7},{4,6},{5,1},{6,4},{7,3},{8,10},{9,13},{10,... | collective-permute-start | bytes 1572872 | tf_op jit(solution)/shard_map/ppermute | solution.py:81
  32.8 12.4 %collective-permute-start.6 = (bf16[4,2,128,256]{3,2,1,0:T(8,128)(2,1)S(1)}, bf16[4,2,128,256]{3,2,1,0:T(8,128)(2,1)S(1)}, u32[]{:S(2)}, u32[]{:S(2)}) collective-permute-start(bf16[4,2,128,256]{3,2,1,0:T(8,128)(2,1)S(1)} %add_convert_fusion), channel_id=1, source_target_pairs={{0,4},{1,3},{2,6},{3,1},{4,0},{5,7},{6,2},{7,5},{8,12},{9,11},{10,... | collective-permute-start | bytes 1572872 | tf_op jit(solution)/shard_map/ppermute | solution.py:81
  46.0 8.3 %collective-permute-start.7 = (bf16[2,128,256]{2,1,0:T(8,128)(2,1)S(1)}, bf16[2,128,256]{2,1,0:T(8,128)(2,1)S(1)}, u32[]{:S(2)}, u32[]{:S(2)}) collective-permute-start(bf16[2,128,256]{2,1,0:T(8,128)(2,1)S(1)} %get-tuple-element.26), channel_id=1, source_target_pairs={{0,8},{1,9},{2,10},{3,11},{4,12},{5,13},{6,14},{7,15},{8,16},{9,17... | collective-permute-start | bytes 393224 | tf_op jit(solution)/shard_map/ppermute | solution.py:81
  47.6 11.8 %collective-permute-start.8 = (bf16[2,128,256]{2,1,0:T(8,128)(2,1)S(1)}, bf16[2,128,256]{2,1,0:T(8,128)(2,1)S(1)}, u32[]{:S(2)}, u32[]{:S(2)}) collective-permute-start(bf16[2,128,256]{2,1,0:T(8,128)(2,1)S(1)} %get-tuple-element.27), channel_id=1, source_target_pairs={{0,16},{1,17},{2,18},{3,19},{4,20},{5,21},{6,22},{7,23},{8,24},{9,... | collective-permute-start | bytes 393224 | tf_op jit(solution)/shard_map/ppermute | solution.py:81
  50.2 9.2 %collective-permute-start.9 = (bf16[2,128,256]{2,1,0:T(8,128)(2,1)S(1)}, bf16[2,128,256]{2,1,0:T(8,128)(2,1)S(1)}, u32[]{:S(2)}, u32[]{:S(2)}) collective-permute-start(bf16[2,128,256]{2,1,0:T(8,128)(2,1)S(1)} %get-tuple-element.28), channel_id=1, source_target_pairs={{0,24},{1,25},{2,26},{3,27},{4,28},{5,29},{6,30},{7,31},{8,0},{9,1... | collective-permute-start | bytes 393224 | tf_op jit(solution)/shard_map/ppermute | solution.py:81
  59.6 8.3 %collective-permute-start.12 = (bf16[2,128,256]{2,1,0:T(8,128)(2,1)S(1)}, bf16[2,128,256]{2,1,0:T(8,128)(2,1)S(1)}, u32[]{:S(2)}, u32[]{:S(2)}) collective-permute-start(bf16[2,128,256]{2,1,0:T(8,128)(2,1)S(1)} %multiply_convert_fusion), channel_id=1, source_target_pairs={{0,24},{1,25},{2,26},{3,27},{4,28},{5,29},{6,30},{7,31},{8,0},{9,1... | collective-permute-start | bytes 393224 | tf_op jit(solution)/shard_map/ppermute | solution.py:81
  64.0 8.0 %collective-permute-start.10 = (bf16[2,128,256]{2,1,0:T(8,128)(2,1)S(1)}, bf16[2,128,256]{2,1,0:T(8,128)(2,1)S(1)}, u32[]{:S(2)}, u32[]{:S(2)}) collective-permute-start(bf16[2,128,256]{2,1,0:T(8,128)(2,1)S(1)} %multiply_convert_fusion), channel_id=1, source_target_pairs={{0,8},{1,9},{2,10},{3,11},{4,12},{5,13},{6,14},{7,15},{8,16},{9,17... | collective-permute-start | bytes 393224 | tf_op jit(solution)/shard_map/ppermute | solution.py:81
  64.0 12.2 %collective-permute-start.11 = (bf16[2,128,256]{2,1,0:T(8,128)(2,1)S(1)}, bf16[2,128,256]{2,1,0:T(8,128)(2,1)S(1)}, u32[]{:S(2)}, u32[]{:S(2)}) collective-permute-start(bf16[2,128,256]{2,1,0:T(8,128)(2,1)S(1)} %multiply_convert_fusion), channel_id=1, source_target_pairs={{0,16},{1,17},{2,18},{3,19},{4,20},{5,21},{6,22},{7,23},{8,24},{9,... | collective-permute-start | bytes 393224 | tf_op jit(solution)/shard_map/ppermute | solution.py:81
  76.3 14.9 %collective-permute-start.13 = (bf16[4,2,128,256]{3,2,1,0:T(8,128)(2,1)S(1)}, bf16[4,2,128,256]{3,2,1,0:T(8,128)(2,1)S(1)}, u32[]{:S(2)}, u32[]{:S(2)}) collective-permute-start(bf16[4,2,128,256]{3,2,1,0:T(8,128)(2,1)S(1)} %pad_maximum_fusion.own), channel_id=1, source_target_pairs={{0,4},{1,3},{2,6},{3,1},{4,0},{5,7},{6,2},{7,5},{8,12},{9,11},{10,... | collective-permute-start | bytes 1572872 | tf_op jit(solution)/shard_map/ppermute | solution.py:81
  77.9 13.8 %collective-permute-start.16 = (bf16[4,2,128,256]{3,2,1,0:T(8,128)(2,1)S(1)}, bf16[4,2,128,256]{3,2,1,0:T(8,128)(2,1)S(1)}, u32[]{:S(2)}, u32[]{:S(2)}) collective-permute-start(bf16[4,2,128,256]{3,2,1,0:T(8,128)(2,1)S(1)} %pad_maximum_fusion.own), channel_id=1, source_target_pairs={{0,2},{1,5},{2,0},{3,7},{4,6},{5,1},{6,4},{7,3},{8,10},{9,13},{10,... | collective-permute-start | bytes 1572872 | tf_op jit(solution)/shard_map/ppermute | solution.py:81
  91.2 9.2 %collective-permute-start.14 = (bf16[4,2,128,256]{3,2,1,0:T(8,128)(2,1)S(1)}, bf16[4,2,128,256]{3,2,1,0:T(8,128)(2,1)S(1)}, u32[]{:S(2)}, u32[]{:S(2)}) collective-permute-start(bf16[4,2,128,256]{3,2,1,0:T(8,128)(2,1)S(1)} %collective-permute-done.13.own), channel_id=1, source_target_pairs={{0,2},{1,5},{2,0},{3,7},{4,6},{5,1},{6,4},{7,3},{8,10},{9,13},{10,... | collective-permute-start | bytes 1572872 | tf_op jit(solution)/shard_map/ppermute | solution.py:81
  91.2 9.2 %collective-permute-start.18 = (bf16[4,2,128,256]{3,2,1,0:T(8,128)(2,1)S(1)}, bf16[4,2,128,256]{3,2,1,0:T(8,128)(2,1)S(1)}, u32[]{:S(2)}, u32[]{:S(2)}) collective-permute-start(bf16[4,2,128,256]{3,2,1,0:T(8,128)(2,1)S(1)} %pad_maximum_fusion.own), channel_id=1, source_target_pairs={{0,1},{1,0},{2,3},{3,2},{4,5},{5,4},{6,7},{7,6},{8,9},{9,8},{10,11... | collective-permute-start | bytes 1572872 | tf_op jit(solution)/shard_map/ppermute | solution.py:81
  91.2 14.3 %collective-permute-start.19 = (bf16[4,2,128,256]{3,2,1,0:T(8,128)(2,1)S(1)}, bf16[4,2,128,256]{3,2,1,0:T(8,128)(2,1)S(1)}, u32[]{:S(2)}, u32[]{:S(2)}) collective-permute-start(bf16[4,2,128,256]{3,2,1,0:T(8,128)(2,1)S(1)} %collective-permute-done.13.own), channel_id=1, source_target_pairs={{0,1},{1,0},{2,3},{3,2},{4,5},{5,4},{6,7},{7,6},{8,9},{9,8},{10,11... | collective-permute-start | bytes 1572872 | tf_op jit(solution)/shard_map/ppermute | solution.py:81
  91.7 19.4 %collective-permute-start.17 = (bf16[4,2,128,256]{3,2,1,0:T(8,128)(2,1)S(1)}, bf16[4,2,128,256]{3,2,1,0:T(8,128)(2,1)S(1)}, u32[]{:S(2)}, u32[]{:S(2)}) collective-permute-start(bf16[4,2,128,256]{3,2,1,0:T(8,128)(2,1)S(1)} %collective-permute-done.16.own), channel_id=1, source_target_pairs={{0,1},{1,0},{2,3},{3,2},{4,5},{5,4},{6,7},{7,6},{8,9},{9,8},{10,11... | collective-permute-start | bytes 1572872 | tf_op jit(solution)/shard_map/ppermute | solution.py:81
  100.3 16.4 %collective-permute-start.15 = (bf16[4,2,128,256]{3,2,1,0:T(8,128)(2,1)S(1)}, bf16[4,2,128,256]{3,2,1,0:T(8,128)(2,1)S(1)}, u32[]{:S(2)}, u32[]{:S(2)}) collective-permute-start(bf16[4,2,128,256]{3,2,1,0:T(8,128)(2,1)S(1)} %collective-permute-done.14.own), channel_id=1, source_target_pairs={{0,1},{1,0},{2,3},{3,2},{4,5},{5,4},{6,7},{7,6},{8,9},{9,8},{10,11... | collective-permute-start | bytes 1572872 | tf_op jit(solution)/shard_map/ppermute | solution.py:81
